TPU v7x, 32 devices: a whole 2x2x4 slice. The times are simulated.
32 devices in a mesh: fsdp: 8 (over z, y), seq: 4 (over x, core).
Axes of the slice: x: 2, y: 2, z: 4, core: 2. Of those that a mesh axis runs over, the one named last changes fastest.
Arguments:
- tokens: bfloat16 [64, 320, 1024], P('fsdp', 'seq'), may hold values from -6 to 6
- lengths: int32 [64], P('fsdp'), may hold values from 200 to 320, as said below
- attn_gain: bfloat16 [1024], P('fsdp'), may hold values from 0.5 to 1.5
- attn_shift: bfloat16 [1024], P('fsdp'), may hold values from -4 to 4
- attn_weight: bfloat16 [1024, 3072], P('fsdp'), may hold values from -0.1875 to 0.1875
- attn_bias: bfloat16 [2048], P('fsdp'), may hold values from -4 to 4
- out_weight: bfloat16 [1024, 1024], P('fsdp'), may hold values from -0.75 to 0.75
- out_bias: bfloat16 [1024], P('fsdp'), may hold values from -4 to 4
- mlp_gain: bfloat16 [1024], P('fsdp'), may hold values from 0.5 to 1.5
- mlp_shift: bfloat16 [1024], P('fsdp'), may hold values from -4 to 4
- up_weight: bfloat16 [1024, 4096], P('fsdp'), may hold values from -0.1875 to 0.1875
- up_bias: bfloat16 [4096], P('fsdp'), may hold values from -4 to 4
- down_weight: bfloat16 [4096, 1024], P('fsdp'), may hold values from -0.09375 to 0.09375
- down_bias: bfloat16 [1024], P('fsdp'), may hold values from -4 to 4
- cotangent: bfloat16 [64, 320, 1024], P('fsdp', 'seq'), may hold values from -6 to 6
Outputs:
- layer_out: bfloat16 [64, 320, 1024], P('fsdp', 'seq')
- input_grad: bfloat16 [64, 320, 1024], P('fsdp', 'seq')
- attn_gain_grad: float32 [1024], P('fsdp')
- attn_shift_grad: float32 [1024], P('fsdp')
- attn_weight_grad: float32 [1024, 3072], P('fsdp')
- attn_bias_grad: float32 [2048], P('fsdp')
- out_weight_grad: float32 [1024, 1024], P('fsdp')
- out_bias_grad: float32 [1024], P('fsdp')
- mlp_gain_grad: float32 [1024], P('fsdp')
- mlp_shift_grad: float32 [1024], P('fsdp')
- up_weight_grad: float32 [1024, 4096], P('fsdp')
- up_bias_grad: float32 [4096], P('fsdp')
- down_weight_grad: float32 [4096, 1024], P('fsdp')
- down_bias_grad: float32 [1024], P('fsdp')
Inputs may be any that keep to these rules, and one draw needn't show every extreme that they name: `lengths`: valid slots come first in each image; among the 8 images of each index of fsdp one has exactly 320 valid slots; some image has 200.
All inputs are finite; a program needn't handle non-finite values.
Results may differ from a plain program's by a relative error of at most 0.015.
Values may be sent and summed in bfloat16 or wider, within the bound.
No kernel may reach another device: no remote copies, remote signals or barrier semaphores. Data moves between devices by JAX's collectives and lax.ppermute only.
A program may use at most 192 MiB of HBM per device.

v0:
```python
import jax
import jax.numpy as jnp
from jax import lax
from jax.sharding import PartitionSpec as P

HEAD_DIM = 64


epsilon = 1e-06


def layer_stats(values):
    center = values - jnp.mean(values, axis=-1, keepdims=True)
    inv_std = lax.rsqrt(jnp.mean(center * center, axis=-1, keepdims=True) + epsilon)
    return (center * inv_std, inv_std)


def norm_back(grad_norm, gain, normal, inv_std):
    scaled = grad_norm * gain
    return inv_std * (
        scaled
        - jnp.mean(scaled, axis=-1, keepdims=True)
        - normal * jnp.mean(scaled * normal, axis=-1, keepdims=True)
    )


def gelu_slope(values):
    cumul = 0.5 * (1.0 + lax.erf(values * 0.7071067811865476))
    density = jnp.exp(-0.5 * values * values) * 0.3989422804014327
    return cumul + values * density


def masked_scores(query_part, keyset, key_mask):
    score_scale = HEAD_DIM ** (-0.5)
    scores = (
        jnp.einsum("pqhe,pkhe->phqk", query_part, keyset, preferred_element_type=jnp.float32)
        * score_scale
    )
    return jnp.where(key_mask[:, None, None, :], scores, -1000000000.0)


def attend(inputs):
    image_pair, key_mask = inputs
    query_part = image_pair[:, :, 0]
    keyset = image_pair[:, :, 1]
    value_part = image_pair[:, :, 2]
    scores = masked_scores(query_part, keyset, key_mask)
    row_top = jnp.max(scores, axis=-1, keepdims=True)
    exp_scores = jnp.exp(scores - row_top)
    row_total = jnp.sum(exp_scores, axis=-1, keepdims=True)
    probs = (exp_scores / row_total).astype(jnp.bfloat16)
    context = jnp.einsum("phqk,pkhe->pqhe", probs, value_part, preferred_element_type=jnp.float32)
    log_total = (row_top + jnp.log(row_total))[..., 0]
    return (context.astype(jnp.bfloat16), log_total)


def attend_back(inputs):
    image_pair, key_mask, log_total, grad_ctx = inputs
    query_part = image_pair[:, :, 0]
    keyset = image_pair[:, :, 1]
    value_part = image_pair[:, :, 2]
    scores = masked_scores(query_part, keyset, key_mask)
    probs = jnp.exp(scores - log_total[..., None])
    probs_low = probs.astype(jnp.bfloat16)
    grad_value = jnp.einsum(
        "phqk,pqhe->pkhe", probs_low, grad_ctx, preferred_element_type=jnp.float32
    )
    grad_probs = jnp.einsum(
        "pqhe,pkhe->phqk", grad_ctx, value_part, preferred_element_type=jnp.float32
    )
    row_inner = jnp.sum(grad_probs * probs, axis=-1, keepdims=True)
    grad_scores = (probs * (grad_probs - row_inner) * HEAD_DIM ** (-0.5)).astype(jnp.bfloat16)
    grad_query = jnp.einsum(
        "phqk,pkhe->pqhe", grad_scores, keyset, preferred_element_type=jnp.float32
    )
    grad_key = jnp.einsum(
        "phqk,pqhe->pkhe", grad_scores, query_part, preferred_element_type=jnp.float32
    )
    return jnp.stack([grad_query, grad_key, grad_value], axis=2).astype(jnp.bfloat16)


def shards(
    tokens,
    lengths,
    attn_gain,
    attn_shift,
    attn_weight,
    attn_bias,
    out_weight,
    out_bias,
    mlp_gain,
    mlp_shift,
    up_weight,
    up_bias,
    down_weight,
    down_bias,
    cotangent,
):
    model_width = tokens.shape[2]
    group_size = lax.axis_size("seq")
    tokens_here, cotangent_here = (tokens, cotangent)
    image_count = tokens.shape[0]
    local_slots = tokens.shape[1]
    positions = lax.axis_index("seq") * local_slots + jnp.arange(local_slots, dtype=jnp.int32)
    slots_all = local_slots * group_size
    weights_all = (
        lax.all_gather(attn_gain, "fsdp", axis=0, tiled=True),
        lax.all_gather(attn_shift, "fsdp", axis=0, tiled=True),
        lax.all_gather(attn_weight, "fsdp", axis=0, tiled=True),
        lax.all_gather(attn_bias, "fsdp", axis=0, tiled=True),
        lax.all_gather(out_weight, "fsdp", axis=0, tiled=True),
        lax.all_gather(out_bias, "fsdp", axis=0, tiled=True),
        lax.all_gather(mlp_gain, "fsdp", axis=0, tiled=True),
        lax.all_gather(mlp_shift, "fsdp", axis=0, tiled=True),
        lax.all_gather(up_weight, "fsdp", axis=0, tiled=True),
        lax.all_gather(up_bias, "fsdp", axis=0, tiled=True),
        lax.all_gather(down_weight, "fsdp", axis=0, tiled=True),
        lax.all_gather(down_bias, "fsdp", axis=0, tiled=True),
    )
    (
        gain_attn,
        shift_attn,
        qkv_full,
        qv_bias,
        proj_out,
        bias_out,
        gain_mlp,
        shift_mlp,
        up_full,
        bias_up,
        down_full,
        bias_down,
    ) = weights_all
    row_valid = positions[None, :] < lengths[:, None]
    key_valid = jnp.arange(slots_all, dtype=jnp.int32)[None, :] < lengths[:, None]
    token_wide = tokens_here.astype(jnp.float32)
    normal_a, inv_a = layer_stats(token_wide)
    normed_a = (normal_a * gain_attn.astype(jnp.float32) + shift_attn.astype(jnp.float32)).astype(
        jnp.bfloat16
    )
    bias_wide = qv_bias.astype(jnp.float32)
    bias_joint = jnp.concatenate(
        [bias_wide[:model_width], jnp.zeros((model_width,), jnp.float32), bias_wide[model_width:]]
    )
    joint_proj = (
        jnp.dot(normed_a, qkv_full, preferred_element_type=jnp.float32) + bias_joint
    ).astype(jnp.bfloat16)
    joint_proj = joint_proj.reshape(image_count, local_slots, 3, model_width)
    heads_joint = lax.all_to_all(joint_proj, "seq", split_axis=3, concat_axis=1, tiled=True)
    head_width = heads_joint.shape[3]
    local_heads = head_width // HEAD_DIM
    pair_size = 2
    step_count = image_count // pair_size
    pairs = heads_joint.reshape(step_count, pair_size, slots_all, 3, local_heads, HEAD_DIM)
    pair_masks = key_valid.reshape(step_count, pair_size, slots_all)
    contexts, log_totals = lax.map(attend, (pairs, pair_masks))
    context_heads = contexts.reshape(image_count, slots_all, head_width)
    context_tok = lax.all_to_all(context_heads, "seq", split_axis=1, concat_axis=2, tiled=True)
    branch = jnp.dot(context_tok, proj_out, preferred_element_type=jnp.float32) + bias_out.astype(
        jnp.float32
    )
    middle = token_wide + branch
    normal_b, inv_b = layer_stats(middle)
    normed_b = (normal_b * gain_mlp.astype(jnp.float32) + shift_mlp.astype(jnp.float32)).astype(
        jnp.bfloat16
    )
    hidden_pre = jnp.dot(normed_b, up_full, preferred_element_type=jnp.float32) + bias_up.astype(
        jnp.float32
    )
    hidden = jax.nn.gelu(hidden_pre, approximate=False).astype(jnp.bfloat16)
    result = (
        middle
        + jnp.dot(hidden, down_full, preferred_element_type=jnp.float32)
        + bias_down.astype(jnp.float32)
    )
    layer_out = jnp.where(row_valid[:, :, None], result, 0.0).astype(jnp.bfloat16)
    weights_back = (
        lax.all_gather(attn_gain, "fsdp", axis=0, tiled=True),
        lax.all_gather(attn_shift, "fsdp", axis=0, tiled=True),
        lax.all_gather(attn_weight, "fsdp", axis=0, tiled=True),
        lax.all_gather(attn_bias, "fsdp", axis=0, tiled=True),
        lax.all_gather(out_weight, "fsdp", axis=0, tiled=True),
        lax.all_gather(out_bias, "fsdp", axis=0, tiled=True),
        lax.all_gather(mlp_gain, "fsdp", axis=0, tiled=True),
        lax.all_gather(mlp_shift, "fsdp", axis=0, tiled=True),
        lax.all_gather(up_weight, "fsdp", axis=0, tiled=True),
        lax.all_gather(up_bias, "fsdp", axis=0, tiled=True),
        lax.all_gather(down_weight, "fsdp", axis=0, tiled=True),
        lax.all_gather(down_bias, "fsdp", axis=0, tiled=True),
    )
    (
        gain_attn,
        shift_attn,
        qkv_full,
        qv_bias,
        proj_out,
        bias_out,
        gain_mlp,
        shift_mlp,
        up_full,
        bias_up,
        down_full,
        bias_down,
    ) = weights_back
    grad_out = jnp.where(row_valid[:, :, None], cotangent_here, jnp.zeros_like(cotangent_here))
    grad_out_wide = grad_out.astype(jnp.float32)
    down_bias_grad = jnp.sum(grad_out_wide, axis=(0, 1))
    down_weight_grad = jnp.einsum(
        "bsf,bsd->fd", hidden, grad_out, preferred_element_type=jnp.float32
    )
    grad_hidden = jnp.einsum("bsd,fd->bsf", grad_out, down_full, preferred_element_type=jnp.float32)
    grad_pre = (grad_hidden * gelu_slope(hidden_pre)).astype(jnp.bfloat16)
    up_bias_grad = jnp.sum(grad_pre.astype(jnp.float32), axis=(0, 1))
    up_weight_grad = jnp.einsum(
        "bsd,bsf->df", normed_b, grad_pre, preferred_element_type=jnp.float32
    )
    grad_normed_b = jnp.einsum("bsf,df->bsd", grad_pre, up_full, preferred_element_type=jnp.float32)
    mlp_gain_grad = jnp.sum(grad_normed_b * normal_b, axis=(0, 1))
    mlp_shift_grad = jnp.sum(grad_normed_b, axis=(0, 1))
    grad_middle = grad_out_wide + norm_back(
        grad_normed_b, gain_mlp.astype(jnp.float32), normal_b, inv_b
    )
    grad_branch = grad_middle.astype(jnp.bfloat16)
    out_bias_grad = jnp.sum(grad_branch.astype(jnp.float32), axis=(0, 1))
    out_weight_grad = jnp.einsum(
        "bsc,bsd->cd", context_tok, grad_branch, preferred_element_type=jnp.float32
    )
    grad_context = jnp.einsum(
        "bsd,cd->bsc", grad_branch, proj_out, preferred_element_type=jnp.float32
    ).astype(jnp.bfloat16)
    grad_context_heads = lax.all_to_all(
        grad_context, "seq", split_axis=2, concat_axis=1, tiled=True
    )
    grad_ctx_pairs = grad_context_heads.reshape(
        step_count, pair_size, slots_all, local_heads, HEAD_DIM
    )
    grad_pairs = lax.map(attend_back, (pairs, pair_masks, log_totals, grad_ctx_pairs))
    grad_heads = grad_pairs.reshape(image_count, slots_all, 3, head_width)
    grad_joint = lax.all_to_all(grad_heads, "seq", split_axis=1, concat_axis=3, tiled=True)
    grad_joint = grad_joint.reshape(image_count, local_slots, 3 * model_width)
    joint_sums = jnp.sum(grad_joint.astype(jnp.float32), axis=(0, 1))
    attn_bias_grad = jnp.concatenate([joint_sums[:model_width], joint_sums[2 * model_width :]])
    attn_weight_grad = jnp.einsum(
        "bsd,bsj->dj", normed_a, grad_joint, preferred_element_type=jnp.float32
    )
    grad_normed_a = jnp.einsum(
        "bsj,dj->bsd", grad_joint, qkv_full, preferred_element_type=jnp.float32
    )
    attn_gain_grad = jnp.sum(grad_normed_a * normal_a, axis=(0, 1))
    attn_shift_grad = jnp.sum(grad_normed_a, axis=(0, 1))
    input_grad = (
        grad_middle + norm_back(grad_normed_a, gain_attn.astype(jnp.float32), normal_a, inv_a)
    ).astype(jnp.bfloat16)
    grad_shards = (
        lax.psum_scatter(attn_gain_grad, "fsdp", scatter_dimension=0, tiled=True),
        lax.psum_scatter(attn_shift_grad, "fsdp", scatter_dimension=0, tiled=True),
        lax.psum_scatter(attn_weight_grad, "fsdp", scatter_dimension=0, tiled=True),
        lax.psum_scatter(attn_bias_grad, "fsdp", scatter_dimension=0, tiled=True),
        lax.psum_scatter(out_weight_grad, "fsdp", scatter_dimension=0, tiled=True),
        lax.psum_scatter(out_bias_grad, "fsdp", scatter_dimension=0, tiled=True),
        lax.psum_scatter(mlp_gain_grad, "fsdp", scatter_dimension=0, tiled=True),
        lax.psum_scatter(mlp_shift_grad, "fsdp", scatter_dimension=0, tiled=True),
        lax.psum_scatter(up_weight_grad, "fsdp", scatter_dimension=0, tiled=True),
        lax.psum_scatter(up_bias_grad, "fsdp", scatter_dimension=0, tiled=True),
        lax.psum_scatter(down_weight_grad, "fsdp", scatter_dimension=0, tiled=True),
        lax.psum_scatter(down_bias_grad, "fsdp", scatter_dimension=0, tiled=True),
    )
    grad_list = tuple(
        (
            lax.psum(grad_shards[0].astype(jnp.bfloat16), "seq").astype(jnp.float32),
            lax.psum(grad_shards[1].astype(jnp.bfloat16), "seq").astype(jnp.float32),
            lax.psum(grad_shards[2].astype(jnp.bfloat16), "seq").astype(jnp.float32),
            lax.psum(grad_shards[3].astype(jnp.bfloat16), "seq").astype(jnp.float32),
            lax.psum(grad_shards[4].astype(jnp.bfloat16), "seq").astype(jnp.float32),
            lax.psum(grad_shards[5].astype(jnp.bfloat16), "seq").astype(jnp.float32),
            lax.psum(grad_shards[6].astype(jnp.bfloat16), "seq").astype(jnp.float32),
            lax.psum(grad_shards[7].astype(jnp.bfloat16), "seq").astype(jnp.float32),
            lax.psum(grad_shards[8].astype(jnp.bfloat16), "seq").astype(jnp.float32),
            lax.psum(grad_shards[9].astype(jnp.bfloat16), "seq").astype(jnp.float32),
            lax.psum(grad_shards[10].astype(jnp.bfloat16), "seq").astype(jnp.float32),
            lax.psum(grad_shards[11].astype(jnp.bfloat16), "seq").astype(jnp.float32),
        )
    )
    return (
        layer_out,
        input_grad,
        grad_list[0],
        grad_list[1],
        grad_list[2],
        grad_list[3],
        grad_list[4],
        grad_list[5],
        grad_list[6],
        grad_list[7],
        grad_list[8],
        grad_list[9],
        grad_list[10],
        grad_list[11],
    )


def solution(mesh):
    return jax.shard_map(
        shards,
        mesh=mesh,
        in_specs=(
            P("fsdp", "seq", None),
            P("fsdp"),
            P("fsdp"),
            P("fsdp"),
            P("fsdp", None),
            P("fsdp"),
            P("fsdp", None),
            P("fsdp"),
            P("fsdp"),
            P("fsdp"),
            P("fsdp", None),
            P("fsdp"),
            P("fsdp", None),
            P("fsdp"),
            P("fsdp", "seq", None),
        ),
        out_specs=(
            P("fsdp", "seq", None),
            P("fsdp", "seq", None),
            P("fsdp"),
            P("fsdp"),
            P("fsdp", None),
            P("fsdp"),
            P("fsdp", None),
            P("fsdp"),
            P("fsdp"),
            P("fsdp"),
            P("fsdp", None),
            P("fsdp"),
            P("fsdp", None),
            P("fsdp"),
        ),
        check_vma=False,
    )
```

profile of v0, /device:TPU:0, one launch (start us, length us, event | category | flops | bytes accessed | tf_op | source)
XLA Modules:
  0.0 1532.3 jit_solution(10418602963580974450)
XLA Ops:
  10.6 22.5 %all-gather.2 = bf16[8,1,256]{2,1,0:T(2,128)(2,1)S(1)} all-gather(bf16[1,1,256]{2,1,0:T(2,128)(2,1)S(1)} %reshape.228), channel_id=1, replica_groups=mesh['fsdp'=8,'seq'=4] {'fsdp'}, dimensions={0}, use_global_device_ids=true | all-gather | bytes 4608 | tf_op jit(solution)/shard_map/all_gather | solution.py:110
  33.1 16.6 %all-gather.1 = bf16[8,1,128]{2,1,0:T(2,128)(2,1)S(1)} all-gather(bf16[1,1,128]{2,1,0:T(2,128)(2,1)} %bitcast.227), channel_id=1, replica_groups=mesh['fsdp'=8,'seq'=4] {'fsdp'}, dimensions={0}, use_global_device_ids=true | all-gather | bytes 2304 | tf_op jit(solution)/shard_map/all_gather | solution.py:108
  49.8 18.5 %all-gather = bf16[8,1,128]{2,1,0:T(2,128)(2,1)S(1)} all-gather(bf16[1,1,128]{2,1,0:T(2,128)(2,1)} %bitcast.228), channel_id=1, replica_groups=mesh['fsdp'=8,'seq'=4] {'fsdp'}, dimensions={0}, use_global_device_ids=true | all-gather | bytes 2304 | tf_op jit(solution)/shard_map/all_gather | solution.py:107
  69.1 43.0 %all-gather.13.cloned.1.call-done = bf16[1024,3072]{1,0:T(8,128)(2,1)} async-done(((bf16[128,3072]{1,0:T(8,128)(2,1)}), bf16[1024,3072]{1,0:T(8,128)(2,1)}) %all-gather.13.cloned.1.call-update) | async-done | bytes 6291472 | tf_op jit(solution)/shard_map/all_gather | solution.py:109
  112.1 8.7 add_convert_fusion
  120.8 12.2 reshape.218
  133.0 9.0 copy.84
  142.0 5.7 all-to-all-start
  148.5 69.9 %all-to-all-done = bf16[8,80,3,1024]{1,0,2,3:T(8,128)(2,1)} async-done(((bf16[8,80,3,1024]{1,0,2,3:T(8,128)(2,1)}), bf16[8,80,3,1024]{1,0,2,3:T(8,128)(2,1)}, u32[]{:S(2)}, u32[]{:S(2)}) %all-to-all-start) | async-done | bytes 3932192 | tf_op jit(solution)/shard_map/all_to_all | solution.py:149
  218.4 10.2 copy.113
  228.7 10.8 reshape.219
  239.4 5.3 copy.87
  244.8 24.1 %while.22 = (s32[]{:T(128)}, bf16[4,2,320,4,64]{2,4,3,1,0:T(8,128)(2,1)S(1)}, f32[4,2,4,320]{3,2,1,0:T(4,128)}, bf16[4,2,320,3,4,64]{2,5,4,1,3,0:T(8,128)(2,1)}, pred[4,2,320]{2,1,0:T(4,128)(4,1)}, /*index=5*/s32[]{:T(128)}) while((s32[]{:T(128)}, bf16[4,2,320,4,64]{2,4,3,1,0:T(8,128)(2,1)S(1)}, f32[4,2,4,320]{3,2,1,0:T(4,128)}, ...), condition=%wide.region_5.6_spmd, body=%wide.region_2.5_spmd.sunk | while | flops 219706880 | bytes 14117853 | solution.py:156
  270.7 3.5 all-to-all-start.1
  274.2 17.9 %all-gather.3 = bf16[8,1,128]{2,1,0:T(2,128)(2,1)S(1)} all-gather(bf16[1,1,128]{2,1,0:T(2,128)(2,1)S(1)} %bitcast.229), channel_id=1, replica_groups=mesh['fsdp'=8,'seq'=4] {'fsdp'}, dimensions={0}, use_global_device_ids=true | all-gather | bytes 2304 | tf_op jit(solution)/shard_map/all_gather | solution.py:112
  292.1 26.6 %all-gather.6 = bf16[8,1,512]{2,1,0:T(2,128)(2,1)S(1)} all-gather(bf16[1,1,512]{2,1,0:T(2,128)(2,1)S(1)} %reshape.236), channel_id=1, replica_groups=mesh['fsdp'=8,'seq'=4] {'fsdp'}, dimensions={0}, use_global_device_ids=true | all-gather | bytes 9216 | tf_op jit(solution)/shard_map/all_gather | solution.py:116
  318.7 16.4 %all-gather.5 = bf16[8,1,128]{2,1,0:T(2,128)(2,1)S(1)} all-gather(bf16[1,1,128]{2,1,0:T(2,128)(2,1)S(1)} %bitcast.230), channel_id=1, replica_groups=mesh['fsdp'=8,'seq'=4] {'fsdp'}, dimensions={0}, use_global_device_ids=true | all-gather | bytes 2304 | tf_op jit(solution)/shard_map/all_gather | solution.py:114
  335.2 18.8 %all-gather.4 = bf16[8,1,128]{2,1,0:T(2,128)(2,1)S(1)} all-gather(bf16[1,1,128]{2,1,0:T(2,128)(2,1)S(1)} %bitcast.231), channel_id=1, replica_groups=mesh['fsdp'=8,'seq'=4] {'fsdp'}, dimensions={0}, use_global_device_ids=true | all-gather | bytes 2304 | tf_op jit(solution)/shard_map/all_gather | solution.py:113
  356.9 4.0 fusion.120
  361.3 16.0 %fusion.99 = (u8[80,4096]{1,0:T(8,128)(4,1)}, u8[80,4096]{1,0:T(8,128)(4,1)}, f32[8,80,4096]{2,1,0:T(8,128)}) fusion(f32[4096]{0:T(1024)S(1)} %bitcast.218, bf16[1024,4096]{1,0:T(8,128)(2,1)} %all-gather.17.cloned.1.call-done, f32[8,80,1024]{2,1,0:T(8,128)S(1)} %get-tuple-element.183, f32[1024]{0:T(1024)S(1)} %bitcast.216, f32[1024]{0:T(1024)S(1)} %bitcast.210, ...), kind=kOutput, calls=%fused_computation.129 | convolution fusion | flops 5408030720 | bytes 22180864 | tf_op jit(solution)/shard_map/dot_general | solution.py:167
  377.3 35.3 %all-gather.19.cloned.1.call-done = bf16[4096,1024]{1,0:T(8,128)(2,1)} async-done(((bf16[512,1024]{1,0:T(8,128)(2,1)}), bf16[4096,1024]{1,0:T(8,128)(2,1)}) %all-gather.19.cloned.1.call-update) | async-done | bytes 8388624 | tf_op jit(solution)/shard_map/all_gather | solution.py:117
  412.6 13.4 convert_reduce_fusion
  426.1 6.6 multiply_reduce_fusion.1
  436.3 2.6 fusion.106
  438.9 4.1 copy.91
  443.0 4.5 all-to-all-start.2
  447.6 5.2 convolution_bitcast_fusion.3
  452.8 20.5 %all-to-all-done.2 = bf16[8,80,1024]{1,0,2:T(8,128)(2,1)} async-done(((bf16[8,80,1024]{1,0,2:T(8,128)(2,1)}), bf16[8,80,1024]{1,0,2:T(8,128)(2,1)}, u32[]{:S(2)}, u32[]{:S(2)}) %all-to-all-start.2) | async-done | bytes 1310752 | tf_op jit(solution)/shard_map/all_to_all | solution.py:231
  473.3 4.5 copy.114
  477.8 3.7 reshape.221
  481.5 106.3 %while.23 = (s32[]{:T(128)}, bf16[4,2,320,3,4,64]{2,5,4,3,1,0:T(8,128)(2,1)}, bf16[4,2,320,3,4,64]{2,5,4,1,3,0:T(8,128)(2,1)}, pred[4,2,320]{2,1,0:T(4,128)(4,1)...) while((s32[]{:T(128)}, bf16[4,2,320,3,4,64]{2,5,4,3,1,0:T(8,128)(2,1)}, ...), condition=%wide.region_12.13_spmd, body=%wide.region_10.12_spmd.sunk | while | flops 537237120 | bytes 63015816 | solution.py:237
  488.3 2.6 fusion.150
  490.9 7.1 fusion.151
  498.0 7.9 fusion.152
  514.8 2.6 fusion.150
  517.5 7.1 fusion.151
  524.6 7.9 fusion.152
  541.4 2.6 fusion.150
  544.1 7.1 fusion.151
  551.2 7.9 fusion.152
  568.0 2.6 fusion.150
  570.6 7.1 fusion.151
  577.7 7.9 fusion.152
  587.8 6.8 copy.95
  594.7 49.1 %all_to_all.63 = bf16[8,320,3,256]{3,0,2,1:T(8,128)(2,1)S(1)} all-to-all(bf16[8,320,3,256]{3,0,2,1:T(8,128)(2,1)} %copy.95), channel_id=1, replica_groups=mesh['fsdp'=8,'seq'=4] {'seq'}, dimensions={1} | all-to-all | bytes 7864320 | tf_op jit(solution)/shard_map/all_to_all | solution.py:239
  645.7 5.0 copy.97
  650.8 7.9 reshape.223
  658.7 10.3 convolution_bitcast_fusion.2
  670.7 12.9 convolution_bitcast_fusion.1
  684.7 25.4 %fusion.54 = bf16[8,80,4096]{2,1,0:T(8,128)(2,1)S(1)} fusion(f32[8,80,4096]{2,1,0:T(8,128)} %get-tuple-element.184, f32[4096]{0:T(1024)S(1)} %bitcast.220, u8[80,4096]{1,0:T(8,128)(4,1)S(1)} %copy-done.24, u8[80,4096]{1,0:T(8,128)(4,1)S(1)} %copy-done.23), kind=kLoop, calls=%fused_computation.58 | loop fusion | flops 186122240 | bytes 16400384 | tf_op jit(solution)/shard_map/convert_element_type | solution.py:170
  712.5 10.6 convolution_bitcast_fusion
  723.7 17.7 %all-gather.7 = bf16[8,1,128]{2,1,0:T(2,128)(2,1)S(1)} all-gather(bf16[1,1,128]{2,1,0:T(2,128)(2,1)S(1)} %bitcast.232), channel_id=1, replica_groups=mesh['fsdp'=8,'seq'=4] {'fsdp'}, dimensions={0}, use_global_device_ids=true | all-gather | bytes 2304 | tf_op jit(solution)/shard_map/all_gather | solution.py:118
  744.0 10.8 select_convert_fusion
  758.1 115.6 %reduce-scatter.5.cloned.1.call-done = f32[128,3072]{1,0:T(8,128)} async-done(((f32[1024,3072]{1,0:T(8,128)}), f32[128,3072]{1,0:T(8,128)}) %reduce-scatter.5.cloned.1.call-update) | async-done | bytes 1572880 | tf_op jit(solution)/shard_map/reduce_scatter | solution.py:257
  876.0 283.3 %reduce-scatter.9.cloned.1.call-done = f32[128,4096]{1,0:T(8,128)} async-done(((f32[1024,4096]{1,0:T(8,128)}), f32[128,4096]{1,0:T(8,128)}) %reduce-scatter.9.cloned.1.call-update) | async-done | bytes 2097168 | tf_op jit(solution)/shard_map/reduce_scatter | solution.py:263
  1159.3 2.7 convert_element_type.201
  1162.0 282.6 %reduce-scatter.11.cloned.1.call-done = f32[512,1024]{1,0:T(8,128)} async-done(((f32[4096,1024]{1,0:T(8,128)}), f32[512,1024]{1,0:T(8,128)}) %reduce-scatter.11.cloned.1.call-update) | async-done | bytes 2097168 | tf_op jit(solution)/shard_map/reduce_scatter | solution.py:265
  1444.6 2.7 convert_element_type.206
  1447.4 10.1 fusion.96
  1457.5 35.7 %all-reduce.8 = (bf16[1024]{0:T(1024)(128)(2,1)S(1)}, bf16[1024]{0:T(1024)(128)(2,1)S(1)}, bf16[2048]{0:T(1024)(128)(2,1)S(1)}, bf16[1024]{0:T(1024)(128)(2,1)S(...) all-reduce(f32[1024]{0:T(1024)S(1)} %get-tuple-element.125, ...), channel_id=2, replica_groups=mesh['fsdp'=8,'seq'=4] {'fsdp'}, use_global_device_ids=true, to_apply=%region_16.17.clone | all-reduce | flops 12288 | bytes 73728
  1493.8 6.4 all-reduce.9
  1504.5 3.9 fusion.95
  1508.3 8.6 all-reduce.13.cloned.1.call-done
  1521.2 2.8 convert_element_type.202
  (223 shorter events, 98.2 us)
Async XLA Ops:
  7.2 61.1 %copy-start.5 = (bf16[8,80,1024]{2,1,0:T(8,128)(2,1)S(1)}, bf16[8,80,1024]{2,1,0:T(8,128)(2,1)}, u32[]{:S(2)}) copy-start(bf16[8,80,1024]{2,1,0:T(8,128)(2,1)} %param.19) | copy-start | bytes 3932164
  7.2 104.9 %all-gather.13.cloned.1.call-start = ((), (), s32[]{:S(2)}) async-start(), calls=%async_computation.8 | async-start | bytes 7077888 | tf_op jit(solution)/shard_map/all_gather | solution.py:109
  7.9 348.9 %all-gather.15.cloned.1.call-start = ((), (), s32[]{:S(2)}) async-start(), calls=%async_computation.9 | async-start | bytes 2359296 | tf_op jit(solution)/shard_map/all_gather | solution.py:111
  8.7 352.7 %all-gather.17.cloned.1.call-start = ((), (), s32[]{:S(2)}) async-start(), calls=%async_computation.10 | async-start | bytes 9437184 | tf_op jit(solution)/shard_map/all_gather | solution.py:115
  9.4 403.2 %all-gather.19.cloned.1.call-start = ((), (), s32[]{:S(2)}) async-start(), calls=%async_computation.11 | async-start | bytes 9437184 | tf_op jit(solution)/shard_map/all_gather | solution.py:117
  49.8 71.1 %copy-start.21 = (f32[8,1,128]{2,1,0:T(1,128)}, f32[8,1,128]{2,1,0:T(1,128)S(1)}, u32[]{:S(2)}) copy-start(f32[8,1,128]{2,1,0:T(1,128)S(1)} %convert_element_type.211) | copy-start | bytes 12292
  68.3 52.6 %copy-start.17 = (f32[8,1,128]{2,1,0:T(1,128)}, f32[8,1,128]{2,1,0:T(1,128)S(1)}, u32[]{:S(2)}) copy-start(f32[8,1,128]{2,1,0:T(1,128)S(1)} %convert_element_type.210) | copy-start | bytes 12292
  68.5 52.3 %copy-start.15 = (f32[8,80]{1,0:T(8,128)}, f32[8,80]{1,0:T(8,128)S(1)}, u32[]{:S(2)}) copy-start(f32[8,80]{1,0:T(8,128)S(1)} %broadcast_multiply_fusion.5) | copy-start | bytes 7684
  69.1 51.7 %copy-start.19 = (f32[8,80]{1,0:T(8,128)}, f32[8,80]{1,0:T(8,128)S(1)}, u32[]{:S(2)}) copy-start(f32[8,80]{1,0:T(8,128)S(1)} %add_rsqrt_fusion.1) | copy-start | bytes 7684
  142.0 5.8 copy-start.34
  142.0 76.4 %all-to-all-start = ((bf16[8,80,3,1024]{1,0,2,3:T(8,128)(2,1)}), bf16[8,80,3,1024]{1,0,2,3:T(8,128)(2,1)}, u32[]{:S(2)}, u32[]{:S(2)}) async-start(bf16[8,80,3,1024]{1,0,2,3:T(8,128)(2,1)} %copy.84), calls=%async_computation | async-start | bytes 12582912 | tf_op jit(solution)/shard_map/all_to_all | solution.py:149
  268.8 5.4 copy-start.36
  268.8 23.3 %copy-start.35 = (bf16[512]{0:T(512)(128)(2,1)S(1)}, bf16[512]{0:T(512)(128)(2,1)}, u32[]{:S(2)}) copy-start(bf16[512]{0:T(512)(128)(2,1)} %param.30) | copy-start | bytes 3076
  268.8 49.9 %copy-start.37 = (bf16[128]{0:T(256)(128)(2,1)S(1)}, bf16[128]{0:T(256)(128)(2,1)}, u32[]{:S(2)}) copy-start(bf16[128]{0:T(256)(128)(2,1)} %param.28) | copy-start | bytes 772
  268.8 66.3 %copy-start.38 = (bf16[128]{0:T(256)(128)(2,1)S(1)}, bf16[128]{0:T(256)(128)(2,1)}, u32[]{:S(2)}) copy-start(bf16[128]{0:T(256)(128)(2,1)} %param.27) | copy-start | bytes 772
  270.7 83.4 %all-to-all-start.1 = ((bf16[8,320,256]{2,0,1:T(8,128)(2,1)}), bf16[8,320,256]{2,0,1:T(8,128)(2,1)S(1)}, u32[]{:S(2)}, u32[]{:S(2)}) async-start(bf16[8,320,256]{2,0,1:T(8,128)(2,1)} %copy.88), calls=%async_computation.1 | async-start | bytes 2621440 | tf_op jit(solution)/shard_map/all_to_all | solution.py:158
  318.7 93.9 %copy-start.25 = (f32[8,1,512]{2,1,0:T(1,128)}, f32[8,1,512]{2,1,0:T(1,128)S(1)}, u32[]{:S(2)}) copy-start(f32[8,1,512]{2,1,0:T(1,128)S(1)} %convert_element_type.216) | copy-start | bytes 49156
  354.1 78.6 %copy-start.30 = (pred[8,80]{1,0:T(8,128)(4,1)}, pred[8,80]{1,0:T(8,128)(4,1)S(1)}, u32[]{:S(2)}) copy-start(pred[8,80]{1,0:T(8,128)(4,1)S(1)} %broadcast_compare_fusion) | copy-start | bytes 1924
  360.9 71.8 %copy-start.3 = (f32[8,80,1024]{2,1,0:T(8,128)}, f32[8,80,1024]{2,1,0:T(8,128)S(1)}, u32[]{:S(2)}) copy-start(f32[8,80,1024]{2,1,0:T(8,128)S(1)} %get-tuple-element.183) | copy-start | bytes 7864324
  412.6 13.4 copy-start.40
  426.1 6.6 copy-start.11
  426.1 6.6 copy-start.12
  432.7 3.6 copy-start.41
  434.6 1.7 copy-start.8
  438.9 8.6 copy-start.9
  443.0 30.2 %all-to-all-start.2 = ((bf16[8,80,1024]{1,0,2:T(8,128)(2,1)}), bf16[8,80,1024]{1,0,2:T(8,128)(2,1)}, u32[]{:S(2)}, u32[]{:S(2)}) async-start(bf16[8,80,1024]{1,0,2:T(8,128)(2,1)} %copy.91), calls=%async_computation.2 | async-start | bytes 4194304 | tf_op jit(solution)/shard_map/all_to_all | solution.py:231
  447.5 308.8 %reduce-scatter.7.cloned.1.call-start = ((), (), s32[]{:S(2)}) async-start(), calls=%async_computation.13 | async-start | bytes 4718592 | tf_op jit(solution)/shard_map/reduce_scatter | solution.py:259
  452.7 420.9 %reduce-scatter.5.cloned.1.call-start = ((), (), s32[]{:S(2)}) async-start(), calls=%async_computation.12 | async-start | bytes 14155776 | tf_op jit(solution)/shard_map/reduce_scatter | solution.py:257
  485.5 2.0 copy-start
  512.1 2.0 copy-start
  538.7 2.0 copy-start
  565.2 2.0 copy-start
  643.8 1.9 copy-start.1
  650.7 7.9 copy-start.6
  650.7 7.9 copy-start.16
  650.7 7.9 copy-start.18
  650.7 7.9 copy-start.20
  650.7 7.9 copy-start.22
  669.0 1.7 copy-start.4
  669.0 490.3 %reduce-scatter.9.cloned.1.call-start = ((), (), s32[]{:S(2)}) async-start(), calls=%async_computation.14 | async-start | bytes 18874368 | tf_op jit(solution)/shard_map/reduce_scatter | solution.py:263
  683.7 1.0 copy-start.23
  683.7 1.1 copy-start.24
  683.7 1.1 copy-start.26
  683.7 760.9 %reduce-scatter.11.cloned.1.call-start = ((), (), s32[]{:S(2)}) async-start(), calls=%async_computation.15 | async-start | bytes 18874368 | tf_op jit(solution)/shard_map/reduce_scatter | solution.py:265
  684.7 27.8 %copy-start.13 = (bf16[8,80,1024]{2,1,0:T(8,128)(2,1)S(1)}, bf16[8,80,1024]{2,1,0:T(8,128)(2,1)}, u32[]{:S(2)}) copy-start(bf16[8,80,1024]{2,1,0:T(8,128)(2,1)} %param.33) | copy-start | bytes 3932164
  684.7 27.8 %copy-start.31 = (pred[8,80]{1,0:T(8,128)(4,1)S(1)}, pred[8,80]{1,0:T(8,128)(4,1)}, u32[]{:S(2)}) copy-start(pred[8,80]{1,0:T(8,128)(4,1)} %copy-done.30) | copy-start | bytes 1924
  710.2 2.3 copy-start.10
  723.1 0.7 copy-start.39
  723.1 18.4 %copy-start.42 = (u32[32]{0:T(128)S(1)}, u32[32]{0:T(128)}, u32[]{:S(2)}) copy-start(u32[32]{0:T(128)} %constant.133) | copy-start | bytes 388
  723.1 793.8 %all-reduce.13.cloned.1.call-start = ((), (), s32[]{:S(2)}) async-start(), calls=%async_computation.16 | async-start | bytes 6291456 | tf_op jit(solution)/shard_map/psum | solution.py:272
  744.0 10.8 copy-start.2
  1162.0 285.3 %copy-start.7 = (bf16[8,80,1024]{2,1,0:T(8,128)(2,1)S(1)}, bf16[8,80,1024]{2,1,0:T(8,128)(2,1)}, u32[]{:S(2)}) copy-start(bf16[8,80,1024]{2,1,0:T(8,128)(2,1)} %param.19) | copy-start | bytes 3932164
  1447.3 10.2 copy-start.27
  1447.4 10.2 copy-start.28
  1447.4 10.1 copy-start.29
  1447.4 10.1 copy-start.32
  1447.4 10.1 copy-start.33
  1516.9 7.1 copy-start.14
Sparse Core Ops, SparseCore 0:
  10.2 101.8 all-gather.12
  114.2 47.4 all-gather.14
  163.8 123.3 all-gather.16
  289.3 123.3 all-gather.18
  452.9 86.5 reduce-scatter.6
  669.1 204.4 reduce-scatter.4
  877.9 281.4 reduce-scatter.8
  1163.1 281.4 reduce-scatter.10
  1448.5 68.3 all-reduce.12
where the time goes:
time: 1540 us; the launch traced here: 1530 us
  waiting for transfers between devices  861 us (56%)
  blocking collectives  246 us (16%)
  matrix products  199 us (13%)
  local copies, waits for them, and re-layouts  124 us (8%)
  other arithmetic  71.2 us (5%)
  between operations  16.5 us (1%)
    reduce_scatter x1, waiting for transfers between devices, shards(): lax.psum_scatter(up_weight_grad, 'fsdp', scatter_dimension=0, tiled=True)  283 us
    reduce_scatter x1, waiting for transfers between devices, shards(): lax.psum_scatter(down_weight_grad, 'fsdp', scatter_dimension=0, tiled=True)  283 us
    reduce_scatter x1, waiting for transfers between devices, shards(): lax.psum_scatter(attn_weight_grad, 'fsdp', scatter_dimension=0, tiled=True)  116 us
    all_to_all x1, waiting for transfers between devices, shards(): lax.all_to_all(joint_proj, 'seq', split_axis=3, concat_axis=1, tiled=True)  69.9 us
    all_to_all x1, blocking collectives, shards(): lax.all_to_all(grad_heads, 'seq', split_axis=1, concat_axis=3, tiled=True)  49.1 us
    all_gather x1, waiting for transfers between devices, shards(): lax.all_gather(attn_weight, 'fsdp', axis=0, tiled=True)  43 us
    unnamed x1, blocking collectives  35.7 us
    all_gather x1, waiting for transfers between devices, shards(): lax.all_gather(down_weight, 'fsdp', axis=0, tiled=True)  35.3 us
  transfers between devices with their start and end apart: 12, of which 8 were waited for; matrix products, arithmetic and copies ran while one was open for 22% of the time, Pallas kernels for 0%

commit v1 on v0

v1 whole, which is shorter than its diff:
```python
import functools

import jax
import jax.numpy as jnp
from jax import lax
from jax.experimental import pallas as pl
from jax.experimental.pallas import tpu as pltpu
from jax.sharding import PartitionSpec as P

HEAD_DIM = 64
LANES = 128
EPSILON = 1e-06
BF16 = jnp.bfloat16
F32 = jnp.float32
ALL = ("fsdp", "seq")


def layer_stats(values):
    center = values - jnp.mean(values, axis=-1, keepdims=True)
    inv_std = lax.rsqrt(jnp.mean(center * center, axis=-1, keepdims=True) + EPSILON)
    return center * inv_std, inv_std


def norm_back(grad_norm, gain, normal, inv_std):
    scaled = grad_norm * gain
    return inv_std * (
        scaled
        - jnp.mean(scaled, axis=-1, keepdims=True)
        - normal * jnp.mean(scaled * normal, axis=-1, keepdims=True)
    )


def contract(a, b, ca, cb):
    return lax.dot_general(a, b, (((ca,), (cb,)), ((), ())), preferred_element_type=F32)


def head_probs(q, k, head, lane, key_ok):
    q_own = jnp.where(lane == head, q, jnp.zeros_like(q))
    scores = contract(q_own, k, 1, 1) * HEAD_DIM ** (-0.5)
    scores = jnp.where(key_ok, scores, -1000000000.0)
    top = jnp.max(scores, axis=-1, keepdims=True)
    exps = jnp.exp(scores - top)
    return exps * (1.0 / jnp.sum(exps, axis=-1, keepdims=True))


def masks(length, slots):
    lane = lax.broadcasted_iota(jnp.int32, (slots, LANES), 1) // HEAD_DIM
    key_ok = lax.broadcasted_iota(jnp.int32, (slots, slots), 1) < length
    return lane, key_ok


def attend_kernel(len_ref, q_ref, k_ref, v_ref, out_ref):
    q, k, v = q_ref[0], k_ref[0], v_ref[0]
    lane, key_ok = masks(len_ref[pl.program_id(0)], q.shape[0])
    context = jnp.zeros(q.shape, F32)
    for head in range(LANES // HEAD_DIM):
        probs = head_probs(q, k, head, lane, key_ok).astype(BF16)
        context = jnp.where(lane == head, contract(probs, v, 1, 0), context)
    out_ref[0] = context.astype(BF16)


def attend_back_kernel(len_ref, q_ref, k_ref, v_ref, g_ref, dq_ref, dk_ref, dv_ref):
    q, k, v, g = q_ref[0], k_ref[0], v_ref[0], g_ref[0]
    lane, key_ok = masks(len_ref[pl.program_id(0)], q.shape[0])
    dq, dk, dv = (jnp.zeros(q.shape, F32) for _ in range(3))
    for head in range(LANES // HEAD_DIM):
        own = lane == head
        probs = head_probs(q, k, head, lane, key_ok)
        g_own = jnp.where(own, g, jnp.zeros_like(g))
        grad_probs = contract(g_own, v, 1, 1)
        inner = jnp.sum(grad_probs * probs, axis=-1, keepdims=True)
        grad_scores = (probs * (grad_probs - inner) * HEAD_DIM ** (-0.5)).astype(BF16)
        dq = jnp.where(own, contract(grad_scores, k, 1, 0), dq)
        dk = jnp.where(own, contract(grad_scores, q, 0, 0), dk)
        dv = jnp.where(own, contract(probs.astype(BF16), g, 0, 0), dv)
    dq_ref[0], dk_ref[0], dv_ref[0] = dq.astype(BF16), dk.astype(BF16), dv.astype(BF16)


def attention(lengths, joint, grad_context=None):
    images, slots, width = joint.shape[0], joint.shape[1], joint.shape[2] // 3
    pairs = width // LANES
    block = (1, slots, LANES)
    specs = [pl.BlockSpec(block, functools.partial(lambda b, i, h, n: (i, 0, b + h), b * pairs)) for b in range(3)]
    plain = pl.BlockSpec(block, lambda i, h, n: (i, 0, h))
    shape = jax.ShapeDtypeStruct((images, slots, width), BF16)
    back = grad_context is not None
    flops = 2 * images * pairs * 2 * slots * slots * LANES * (5 if back else 2)
    return pl.pallas_call(
        attend_back_kernel if back else attend_kernel,
        grid_spec=pltpu.PrefetchScalarGridSpec(
            num_scalar_prefetch=1,
            grid=(images, pairs),
            in_specs=specs + ([plain] if back else []),
            out_specs=[plain] * 3 if back else plain,
        ),
        out_shape=[shape] * 3 if back else shape,
        cost_estimate=pl.CostEstimate(
            flops=flops,
            bytes_accessed=images * slots * width * 2 * (7 if back else 4),
            transcendentals=images * pairs * 2 * slots * slots,
        ),
    )(lengths, joint, joint, joint, *([grad_context] if back else []))


def gather_weight(weight):
    parts = lax.axis_size("seq")
    rows = weight.shape[0] // parts
    mine = lax.dynamic_slice_in_dim(weight, lax.axis_index("seq") * rows, rows, 0)
    return lax.all_gather(mine, ALL, axis=0, tiled=True)


def scatter_grad(grad):
    mine = lax.psum_scatter(grad, ALL, scatter_dimension=0, tiled=True)
    return lax.all_gather(mine, "seq", axis=0, tiled=True).astype(F32)


def shards(
    tokens,
    lengths,
    attn_gain,
    attn_shift,
    attn_weight,
    attn_bias,
    out_weight,
    out_bias,
    mlp_gain,
    mlp_shift,
    up_weight,
    up_bias,
    down_weight,
    down_bias,
    cotangent,
):
    width = tokens.shape[2]
    members = lax.axis_size("seq")
    images = tokens.shape[0] // members
    slots = tokens.shape[1] * members
    rows = images * slots

    small = (attn_gain, attn_shift, attn_bias, out_bias, mlp_gain, mlp_shift, up_bias, down_bias)
    sizes = [v.shape[0] for v in small]
    small_all = lax.all_gather(jnp.concatenate(small), "fsdp", axis=0).astype(F32)
    cuts = [sum(sizes[:i]) for i in range(len(sizes))]
    gain_a, shift_a, bias_qv, bias_out, gain_b, shift_b, bias_up, bias_down = (
        small_all[:, c : c + n].reshape(-1) for c, n in zip(cuts, sizes)
    )
    qkv_full, out_full, up_full, down_full = (
        gather_weight(w) for w in (attn_weight, out_weight, up_weight, down_weight)
    )

    lens = lax.dynamic_slice_in_dim(lengths, lax.axis_index("seq") * images, images, 0)
    valid = jnp.arange(slots, dtype=jnp.int32)[None, :] < lens[:, None]
    valid = valid.reshape(rows, 1)
    by_image = functools.partial(
        lax.all_to_all, axis_name="seq", split_axis=0, concat_axis=1, tiled=True
    )
    by_slot = functools.partial(
        lax.all_to_all, axis_name="seq", split_axis=1, concat_axis=0, tiled=True
    )
    wide = by_image(tokens).reshape(rows, width).astype(F32)
    cot = by_image(cotangent).reshape(rows, width)

    normal_a, inv_a = layer_stats(wide)
    normed_a = (normal_a * gain_a + shift_a).astype(BF16)
    bias_joint = jnp.concatenate([bias_qv[:width], jnp.zeros((width,), F32), bias_qv[width:]])
    joint = (contract(normed_a, qkv_full, 1, 0) + bias_joint).astype(BF16)
    joint = joint.reshape(images, slots, 3 * width)
    context = attention(lens, joint).reshape(rows, width)
    middle = wide + (contract(context, out_full, 1, 0) + bias_out)
    normal_b, inv_b = layer_stats(middle)
    normed_b = (normal_b * gain_b + shift_b).astype(BF16)
    pre = contract(normed_b, up_full, 1, 0) + bias_up
    cumul = 0.5 * (1.0 + lax.erf(pre * 0.7071067811865476))
    hidden = (pre * cumul).astype(BF16)
    slope = (cumul + pre * jnp.exp(-0.5 * pre * pre) * 0.3989422804014327).astype(BF16)
    result = middle + contract(hidden, down_full, 1, 0) + bias_down
    layer_out = jnp.where(valid, result, 0.0).astype(BF16)
    layer_out = by_slot(layer_out.reshape(images, slots, width))

    grad_out = jnp.where(valid, cot, jnp.zeros_like(cot))
    grad_out_wide = grad_out.astype(F32)
    g_bias_down = jnp.sum(grad_out_wide, axis=0)
    g_down = scatter_grad(contract(hidden, grad_out, 0, 0).astype(BF16))
    grad_pre = (contract(grad_out, down_full, 1, 1) * slope.astype(F32)).astype(BF16)
    g_bias_up = jnp.sum(grad_pre.astype(F32), axis=0)
    g_up = scatter_grad(contract(normed_b, grad_pre, 0, 0).astype(BF16))
    grad_nb = contract(grad_pre, up_full, 1, 1)
    g_gain_b = jnp.sum(grad_nb * normal_b, axis=0)
    g_shift_b = jnp.sum(grad_nb, axis=0)
    grad_middle = grad_out_wide + norm_back(grad_nb, gain_b, normal_b, inv_b)
    grad_branch = grad_middle.astype(BF16)
    g_bias_out = jnp.sum(grad_branch.astype(F32), axis=0)
    g_out = scatter_grad(contract(context, grad_branch, 0, 0).astype(BF16))
    grad_context = contract(grad_branch, out_full, 1, 1).astype(BF16)
    grad_parts = attention(lens, joint, grad_context.reshape(images, slots, width))
    grad_joint = jnp.concatenate(grad_parts, axis=2).reshape(rows, 3 * width)
    joint_sums = jnp.sum(grad_joint.astype(F32), axis=0)
    g_bias_qv = jnp.concatenate([joint_sums[:width], joint_sums[2 * width :]])
    g_qkv = scatter_grad(contract(normed_a, grad_joint, 0, 0).astype(BF16))
    grad_na = contract(grad_joint, qkv_full, 1, 1)
    g_gain_a = jnp.sum(grad_na * normal_a, axis=0)
    g_shift_a = jnp.sum(grad_na, axis=0)
    input_grad = (grad_middle + norm_back(grad_na, gain_a, normal_a, inv_a)).astype(BF16)
    input_grad = by_slot(input_grad.reshape(images, slots, width))

    shard_count = lax.axis_size("fsdp")
    small_grads = (g_gain_a, g_shift_a, g_bias_qv, g_bias_out, g_gain_b, g_shift_b, g_bias_up, g_bias_down)
    packed = jnp.concatenate([v.reshape(shard_count, -1) for v in small_grads], axis=1)
    packed = lax.psum(packed, ALL)
    packed = lax.dynamic_slice_in_dim(packed, lax.axis_index("fsdp"), 1, 0)[0]
    (g_gain_a, g_shift_a, g_bias_qv, g_bias_out, g_gain_b, g_shift_b, g_bias_up, g_bias_down) = (
        packed[c : c + n] for c, n in zip(cuts, sizes)
    )
    return (
        layer_out,
        input_grad,
        g_gain_a,
        g_shift_a,
        g_qkv,
        g_bias_qv,
        g_out,
        g_bias_out,
        g_gain_b,
        g_shift_b,
        g_up,
        g_bias_up,
        g_down,
        g_bias_down,
    )


def solution(mesh):
    rows, vector, matrix = P("fsdp", "seq", None), P("fsdp"), P("fsdp", None)
    weights = (vector, vector, matrix, vector, matrix, vector, vector, vector, matrix, vector, matrix, vector)
    return jax.shard_map(
        shards,
        mesh=mesh,
        in_specs=(rows, vector) + weights + (rows,),
        out_specs=(rows, rows) + weights,
        check_vma=False,
    )
```

time: 1540 us -> 932 us (0.61)
  waiting for transfers between devices: 861 us -> 573 us
  blocking collectives: 246 us -> 98.9 us
  local copies, waits for them, and re-layouts: 124 us -> 33.1 us
  matrix products: 199 us -> 109 us
  Pallas kernels: 0 us -> 48.4 us
  other arithmetic: 71.2 us -> 30.9 us
    reduce_scatter x4, waiting for transfers between devices: 681 us -> 361 us  [scatter_grad(): mine = lax.psum_scatter(grad, ALL, scatter_dimension=0, tiled=True)]
    all_gather x4 -> x6, waiting for transfers between devices: 78.3 us -> 193 us  [the longest x4 170 us: gather_weight(): return lax.all_gather(mine, ALL, axis=0, tiled=True)]
    all_gather x8 -> x3, blocking collectives: 155 us -> 46.7 us  [the longest x1 31.9 us: shards(): lax.all_gather(jnp.concatenate(small), 'fsdp', axis=0).astype(F32)]
    dot_general x40 -> x12, matrix products: 199 us -> 109 us  [contract(): lax.dot_general(a, b, (((ca,), (cb,)), ((), ())), preferred_element_type=...]
    all_to_all x3 -> x4, waiting for transfers between devices: 90.4 us -> 18.6 us  [the longest x1 18.6 us: shards(): cot = by_image(cotangent).reshape(rows, width)]
    all_to_all x1 -> x0, blocking collectives: 49.1 us -> none  [shards(): lax.all_to_all(grad_heads, 'seq', split_axis=1, concat_axis=3, tiled=True)]
    pallas_call x0 -> x2, Pallas kernels: none -> 48.4 us  [attention(): pl.pallas_call(attend_back_kernel if back else attend_kernel, grid_spec=p...]
    reshape x7 -> x3, local copies, waits for them, and re-layouts: 52.3 us -> 6.13 us  [the longest x1 3.72 us: shards(): input_grad = by_slot(input_grad.reshape(images, slots, width))]
  transfers between devices with their start and end apart: 12 -> 14, of which waited for: 8 -> 11; matrix products, arithmetic and copies ran while one was open for 22% -> 15% of each run, Pallas kernels for 0% -> 5%
where the time goes in v1:
time: 932 us; the launch traced here: 925 us
  waiting for transfers between devices  573 us (61%)
  matrix products  109 us (12%)
  blocking collectives  98.9 us (11%)
  Pallas kernels  48.4 us (5%)
  local copies, waits for them, and re-layouts  33.1 us (4%)
  other arithmetic  30.9 us (3%)
  starting transfers between devices  17.2 us (2%)
  between operations  15.1 us (2%)
    reduce_scatter x4, waiting for transfers between devices, scatter_grad(): mine = lax.psum_scatter(grad, ALL, scatter_dimension=0, tiled=True)  361 us
    all_gather x4, waiting for transfers between devices, gather_weight(): return lax.all_gather(mine, ALL, axis=0, tiled=True)  170 us
    dot_general x12, matrix products, contract(): lax.dot_general(a, b, (((ca,), (cb,)), ((), ())), preferred_element_type=...  109 us
    psum x1, blocking collectives, shards(): packed = lax.psum(packed, ALL)  52.2 us
    pallas_call x2, Pallas kernels, attention(): pl.pallas_call(attend_back_kernel if back else attend_kernel, grid_spec=p...  48.4 us
    all_gather x1, blocking collectives, shards(): lax.all_gather(jnp.concatenate(small), 'fsdp', axis=0).astype(F32)  31.9 us
    all_gather x2, waiting for transfers between devices, scatter_grad(): return lax.all_gather(mine, 'seq', axis=0, tiled=True).astype(F32)  22.9 us
  transfers between devices with their start and end apart: 14, of which 11 were waited for; matrix products, arithmetic and copies ran while one was open for 15% of the time, Pallas kernels for 5%

profile of v1, /device:TPU:0, one launch (start us, length us, event | category | flops | bytes accessed | tf_op | source)
XLA Modules:
  0.0 925.2 jit_solution(14064768571111260219)
XLA Ops:
  7.3 1.7 constant_dynamic-slice_fusion.4
  9.0 1.5 constant_dynamic-slice_fusion.3
  10.6 0.7 constant_dynamic-slice_fusion.2
  11.4 1.7 constant_dynamic-slice_fusion.1
  13.2 4.4 all-to-all-start.2
  17.6 18.6 %all-to-all-done.2 = bf16[8,80,1024]{2,1,0:T(8,128)(2,1)S(1)} async-done(((bf16[8,80,1024]{2,1,0:T(8,128)(2,1)}), bf16[8,80,1024]{2,1,0:T(8,128)(2,1)S(1)}, u32[]{:S(2)}, u32[]{:S(2)}) %all-to-all-start.2) | async-done | bytes 1310752 | tf_op jit(solution)/shard_map/all_to_all | solution.py:161
  36.2 4.3 all-to-all-start
  42.5 31.9 %all-gather.1 = bf16[8,1,1536]{2,1,0:T(2,128)(2,1)S(1)} all-gather(bf16[1,1,1536]{2,1,0:T(2,128)(2,1)S(1)} %reshape.242), channel_id=2, replica_groups=mesh['fsdp'=8,'seq'=4] {'fsdp'}, dimensions={0}, use_global_device_ids=true | all-gather | bytes 27648 | tf_op jit(solution)/shard_map/all_gather | solution.py:142
  74.5 1.2 copy.36
  75.7 3.1 copy.33
  78.8 1.6 bitcast_convert_fusion
  81.3 2.7 bitcast_select_fusion
  84.0 1.5 add_convert_fusion.4
  85.5 2.6 all-gather.9.cloned.1.call-done
  88.1 9.3 %add_convert_fusion = bf16[640,3072]{1,0:T(8,128)(2,1)} fusion(bf16[640,1024]{1,0:T(8,128)(2,1)} %add_convert_fusion.4, bf16[1024,3072]{1,0:T(8,128)(2,1)} %all-gather.9.cloned.1.call-done, f32[3072]{0:T(1024)S(1)} %pad_maximum_fusion), kind=kOutput, calls=%fused_computation.11 | convolution fusion | flops 4030464000 | bytes 11546624 | tf_op jit(solution)/shard_map/dot_general | solution.py:34
  97.4 19.6 %shard_map.254 = bf16[2,320,1024]{2,1,0:T(8,128)(2,1)} custom-call(s32[2]{0:T(128)} %copy-done.13, bf16[2,320,3072]{2,1,0:T(8,128)(2,1)} %bitcast.120, bf16[2,320,3072]{2,1,0:T(8,128)(2,1)} %bitcast.121, bf16[2,320,3072]{2,1,0:T(8,128)(2,1)} %bitcast.122), custom_call_target="tpu_custom_call" | custom-call | flops 1677721600 | bytes 5242880 | tf_op jit(solution)/shard_map/pallas_call | solution.py:88
  117.0 28.9 %all-gather.11.cloned.1.call-done = bf16[1024,1024]{1,0:T(8,128)(2,1)} async-done(((bf16[32,1024]{1,0:T(8,128)(2,1)}), bf16[1024,1024]{1,0:T(8,128)(2,1)}) %all-gather.11.cloned.1.call-update) | async-done | bytes 2097168 | tf_op jit(solution)/shard_map/all_gather | solution.py:109
  145.9 5.1 fusion.11
  151.0 2.1 multiply_reduce_fusion.4
  153.1 72.6 %all-gather.13.cloned.1.call-done = bf16[1024,4096]{1,0:T(8,128)(2,1)} async-done(((bf16[32,4096]{1,0:T(8,128)(2,1)}), bf16[1024,4096]{1,0:T(8,128)(2,1)}) %all-gather.13.cloned.1.call-update) | async-done | bytes 8388624 | tf_op jit(solution)/shard_map/all_gather | solution.py:109
  225.7 13.3 %multiply_convert_fusion.1 = (bf16[640,4096]{1,0:T(8,128)(2,1)}, f32[640,4096]{1,0:T(8,128)}) fusion(f32[4096]{0:T(1024)S(1)} %bitcast.141, bf16[1024,4096]{1,0:T(8,128)(2,1)} %all-gather.13.cloned.1.call-done, f32[640,1024]{1,0:T(8,128)} %get-tuple-element.47, f32[1024]{0:T(1024)S(1)} %get-tuple-element.37, f32[1024]{0:T(1024)S(1)} %get-tuple-element.38, ...), kind=kOutput, calls=%fused_computation.8 | convolution fusion | flops 5387714560 | bytes 26768384 | tf_op jit(solution)/shard_map/dot_general | solution.py:34
  239.0 66.1 %all-gather.15.cloned.1.call-done = bf16[4096,1024]{1,0:T(8,128)(2,1)} async-done(((bf16[128,1024]{1,0:T(8,128)(2,1)}), bf16[4096,1024]{1,0:T(8,128)(2,1)}) %all-gather.15.cloned.1.call-update) | async-done | bytes 8388624 | tf_op jit(solution)/shard_map/all_gather | solution.py:109
  305.1 13.2 %convert_reduce_fusion = (f32[4096]{0:T(1024)S(1)}, bf16[640,4096]{1,0:T(8,128)(2,1)S(1)}) fusion(f32[640,4096]{1,0:T(8,128)} %get-tuple-element.49, f32[4096]{0:T(1024)S(1)} %bitcast.142, bf16[640,1024]{1,0:T(8,128)(2,1)} %bitcast_select_fusion, bf16[4096,1024]{1,0:T(8,128)(2,1)} %all-gather.15.cloned.1.call-done), kind=kOutput, calls=%fused_computation.6 | convolution fusion | flops 5408026624 | bytes 25460736 | tf_op jit(solution)/shard_map/dot_general | solution.py:34
  318.3 2.4 copy-done.24
  320.7 11.3 %convolution_convert_fusion = bf16[1024,4096]{1,0:T(8,128)(2,1)} fusion(bf16[640,4096]{1,0:T(8,128)(2,1)S(1)} %get-tuple-element.53, f32[640,1024]{1,0:T(8,128)} %get-tuple-element.47, f32[1024]{0:T(1024)S(1)} %get-tuple-element.37, f32[1024]{0:T(1024)S(1)} %get-tuple-element.38, f32[640]{0:T(1024)S(1)} %add_rsqrt_fusion, f32[640]{0:T(1024)S(1)} %broadcast_multiply_fusion.4), kind=kOutput, calls=%fused_computation.12 | convolution fusion | flops 5376180224 | bytes 16266240 | tf_op jit(solution)/shard_map/dot_general | solution.py:34
  332.1 11.9 %convolution_convert_fusion.1 = bf16[4096,1024]{1,0:T(8,128)(2,1)} fusion(bf16[640,4096]{1,0:T(8,128)(2,1)} %get-tuple-element.48, bf16[640,1024]{1,0:T(8,128)(2,1)} %bitcast_select_fusion), kind=kOutput, calls=%fused_computation.13 | convolution fusion | flops 5372903424 | bytes 14942208 | tf_op jit(solution)/shard_map/dot_general | solution.py:34
  344.1 11.0 %multiply_reduce_fusion = (f32[1024]{0:T(1024)S(1)}, f32[640]{0:T(1024)S(1)}, f32[640]{0:T(1024)S(1)}, f32[1024]{0:T(1024)S(1)}, f32[640,1024]{1,0:T(8,128)S(1)}) fusion(f32[640,1024]{1,0:T(8,128)} %get-tuple-element.47, f32[640]{0:T(1024)S(1)} %add_rsqrt_fusion, f32[640]{0:T(1024)S(1)} %broadcast_multiply_fusion.4, f32[1024]{0:T(1024)S(1)} %get-tuple-element.38, ...), kind=kOutput, calls=%fused_computation.22 | convolution fusion | flops 5374604288 | bytes 18896896 | tf_op jit(solution)/shard_map/dot_general | solution.py:34
  355.1 2.7 convert_reduce_fusion.3
  357.8 1.4 copy-done.5
  359.3 3.2 convolution_convert_fusion.3
  362.5 3.1 add_convert_fusion.1
  365.6 4.2 convolution_convert_fusion.4
  369.9 28.8 %shard_map.255 = (bf16[2,320,1024]{2,1,0:T(8,128)(2,1)}, bf16[2,320,1024]{2,1,0:T(8,128)(2,1)}, bf16[2,320,1024]{2,1,0:T(8,128)(2,1)}) custom-call(s32[2]{0:T(128)} %copy-done.13, bf16[2,320,3072]{2,1,0:T(8,128)(2,1)} %bitcast.123, bf16[2,320,3072]{2,1,0:T(8,128)(2,1)} %bitcast.124, bf16[2,320,3072]{2,1,0:T(8,128)(2,1)} %bitcast.125, ...), custom_call_target="tpu_custom_call" | custom-call | flops 4194304000 | bytes 9175040 | tf_op jit(solution)/shard_map/pallas_call | solution.py:88
  398.7 1.6 constant_dynamic-update-slice_fusion.2
  400.9 1.9 copy-done.7
  402.8 7.1 convolution_convert_fusion.2
  410.0 0.6 copy-done.14
  410.7 1.7 convert_reduce_fusion.2
  412.3 10.0 %select_convert_fusion = bf16[640,1024]{1,0:T(8,128)(2,1)S(1)} fusion(f32[640,1024]{1,0:T(8,128)} %get-tuple-element.47, bf16[640,4096]{1,0:T(8,128)(2,1)} %get-tuple-element.48, bf16[4096,1024]{1,0:T(8,128)(2,1)} %all-gather.15.cloned.1.call-done, f32[1024]{0:T(1024)S(1)} %get-tuple-element.36, pred[640]{0:T(1024)(128)(4,1)S(1)} %lt.53), kind=kOutput, calls=%fused_computation.29 | convolution fusion | flops 5371330560 | bytes 17568384 | tf_op jit(solution)/shard_map/dot_general | solution.py:34
  422.3 2.4 copy.34
  424.7 4.3 all-to-all-start.1
  429.4 3.1 convert_reduce_fusion.1
  432.7 9.0 multiply_reduce_fusion.1
  441.7 38.0 %reduce-scatter.9.cloned.1.call-done = bf16[32,4096]{1,0:T(8,128)(2,1)} async-done(((bf16[1024,4096]{1,0:T(8,128)(2,1)}), bf16[32,4096]{1,0:T(8,128)(2,1)}) %reduce-scatter.9.cloned.1.call-update) | async-done | bytes 262160 | tf_op jit(solution)/shard_map/reduce_scatter | solution.py:113
  479.9 3.8 add_convert_fusion.2
  483.7 143.1 %reduce-scatter.11.cloned.1.call-done = bf16[128,1024]{1,0:T(8,128)(2,1)} async-done(((bf16[4096,1024]{1,0:T(8,128)(2,1)}), bf16[128,1024]{1,0:T(8,128)(2,1)}) %reduce-scatter.11.cloned.1.call-update) | async-done | bytes 262160 | tf_op jit(solution)/shard_map/reduce_scatter | solution.py:113
  626.9 3.7 copy.37
  630.6 3.5 all-to-all-start.3
  634.2 52.2 %psum.7 = f32[8,1536]{1,0:T(8,128)S(1)} all-reduce(f32[8,1536]{1,0:T(8,128)S(1)} %constant_dynamic-update-slice_fusion.3), channel_id=1, replica_groups=mesh['fsdp'=8,'seq'=4] {'fsdp','seq'}, use_global_device_ids=true, to_apply=%region_16.17 | all-reduce | flops 12288 | bytes 98304 | tf_op jit(solution)/shard_map/psum | solution.py:209
  686.4 0.6 dynamic-slice.2
  687.1 0.7 dynamic-slice.6
  687.7 0.6 dynamic-slice_bitcast_fusion
  688.3 2.7 copy.35
  691.1 1.4 copy.38
  692.5 70.1 %reduce-scatter.7.cloned.1.call-done = bf16[32,1024]{1,0:T(8,128)(2,1)} async-done(((bf16[1024,1024]{1,0:T(8,128)(2,1)}), bf16[32,1024]{1,0:T(8,128)(2,1)}) %reduce-scatter.7.cloned.1.call-update) | async-done | bytes 65552 | tf_op jit(solution)/shard_map/reduce_scatter | solution.py:113
  762.6 6.0 all_gather.37
  768.6 0.8 convert_element_type.127
  769.4 110.0 %reduce-scatter.5.cloned.1.call-done = bf16[32,3072]{1,0:T(8,128)(2,1)} async-done(((bf16[1024,3072]{1,0:T(8,128)(2,1)}), bf16[32,3072]{1,0:T(8,128)(2,1)}) %reduce-scatter.5.cloned.1.call-update) | async-done | bytes 196624 | tf_op jit(solution)/shard_map/reduce_scatter | solution.py:113
  879.4 8.8 all_gather.36
  888.2 1.3 convert_element_type.125
  889.5 7.5 all-gather.17.cloned.1.call-done
  896.9 2.8 convert_element_type.129
  899.7 15.4 %all-gather.19.cloned.1.call-done = bf16[512,1024]{1,0:T(8,128)(2,1)} async-done(((bf16[128,1024]{1,0:T(8,128)(2,1)}), bf16[512,1024]{1,0:T(8,128)(2,1)}) %all-gather.19.cloned.1.call-update) | async-done | bytes 1048592 | tf_op jit(solution)/shard_map/all_gather | solution.py:114
  915.1 2.8 convert_element_type.131
  (117 shorter events, 4.8 us)
Async XLA Ops:
  7.2 3.4 copy-start
  7.2 10.4 %copy-start.23 = (s32[8]{0:T(128)S(1)}, s32[8]{0:T(128)}, u32[]{:S(2)}) copy-start(s32[8]{0:T(128)} %param.16) | copy-start | bytes 100
  7.2 80.9 %all-gather.9.cloned.1.call-start = ((), (), s32[]{:S(2)}) async-start(), calls=%async_computation.8 | async-start | bytes 6488064 | tf_op jit(solution)/shard_map/all_gather | solution.py:109
  9.0 137.0 %all-gather.11.cloned.1.call-start = ((), (), s32[]{:S(2)}) async-start(), calls=%async_computation.9 | async-start | bytes 2162688 | tf_op jit(solution)/shard_map/all_gather | solution.py:109
  10.5 215.2 %all-gather.13.cloned.1.call-start = ((), (), s32[]{:S(2)}) async-start(), calls=%async_computation.10 | async-start | bytes 8650752 | tf_op jit(solution)/shard_map/all_gather | solution.py:109
  11.3 293.7 %all-gather.15.cloned.1.call-start = ((), (), s32[]{:S(2)}) async-start(), calls=%async_computation.11 | async-start | bytes 8650752 | tf_op jit(solution)/shard_map/all_gather | solution.py:109
  13.1 27.7 %copy-start.16 = (bf16[128]{0:T(256)(128)(2,1)S(1)}, bf16[128]{0:T(256)(128)(2,1)}, u32[]{:S(2)}) copy-start(bf16[128]{0:T(256)(128)(2,1)} %param.17) | copy-start | bytes 772
  13.1 27.8 %copy-start.17 = (bf16[128]{0:T(256)(128)(2,1)S(1)}, bf16[128]{0:T(256)(128)(2,1)}, u32[]{:S(2)}) copy-start(bf16[128]{0:T(256)(128)(2,1)} %param.18) | copy-start | bytes 772
  13.1 28.1 %copy-start.18 = (bf16[256]{0:T(256)(128)(2,1)S(1)}, bf16[256]{0:T(256)(128)(2,1)}, u32[]{:S(2)}) copy-start(bf16[256]{0:T(256)(128)(2,1)} %param.20) | copy-start | bytes 1540
  13.1 28.3 %copy-start.19 = (bf16[128]{0:T(256)(128)(2,1)S(1)}, bf16[128]{0:T(256)(128)(2,1)}, u32[]{:S(2)}) copy-start(bf16[128]{0:T(256)(128)(2,1)} %param.22) | copy-start | bytes 772
  13.1 28.5 %copy-start.20 = (bf16[128]{0:T(256)(128)(2,1)S(1)}, bf16[128]{0:T(256)(128)(2,1)}, u32[]{:S(2)}) copy-start(bf16[128]{0:T(256)(128)(2,1)} %param.23) | copy-start | bytes 772
  13.2 28.7 %copy-start.21 = (bf16[128]{0:T(256)(128)(2,1)S(1)}, bf16[128]{0:T(256)(128)(2,1)}, u32[]{:S(2)}) copy-start(bf16[128]{0:T(256)(128)(2,1)} %param.24) | copy-start | bytes 772
  13.2 28.9 %copy-start.15 = (bf16[512]{0:T(512)(128)(2,1)S(1)}, bf16[512]{0:T(512)(128)(2,1)}, u32[]{:S(2)}) copy-start(bf16[512]{0:T(512)(128)(2,1)} %param.26) | copy-start | bytes 3076
  13.2 29.1 %copy-start.22 = (bf16[128]{0:T(256)(128)(2,1)S(1)}, bf16[128]{0:T(256)(128)(2,1)}, u32[]{:S(2)}) copy-start(bf16[128]{0:T(256)(128)(2,1)} %param.28) | copy-start | bytes 772
  13.2 23.0 %all-to-all-start.2 = ((bf16[8,80,1024]{2,1,0:T(8,128)(2,1)}), bf16[8,80,1024]{2,1,0:T(8,128)(2,1)S(1)}, u32[]{:S(2)}, u32[]{:S(2)}) async-start(bf16[8,80,1024]{2,1,0:T(8,128)(2,1)} %param.29), calls=%async_computation.2 | async-start | bytes 2621440 | tf_op jit(solution)/shard_map/all_to_all | solution.py:161
  17.6 58.1 %copy-start.13 = (s32[2]{0:T(128)}, s32[2]{0:T(128)S(1)}, u32[]{:S(2)}) copy-start(s32[2]{0:T(128)S(1)} %dynamic_slice.18.len_ref) | copy-start | bytes 28
  36.2 39.5 %copy-start.3 = (bf16[8,80,1024]{2,1,0:T(8,128)(2,1)}, bf16[8,80,1024]{2,1,0:T(8,128)(2,1)S(1)}, u32[]{:S(2)}) copy-start(bf16[8,80,1024]{2,1,0:T(8,128)(2,1)S(1)} %all-to-all-done.2) | copy-start | bytes 3932164
  36.2 39.5 %all-to-all-start = ((bf16[8,80,1024]{2,1,0:T(8,128)(2,1)}), bf16[8,80,1024]{2,1,0:T(8,128)(2,1)}, u32[]{:S(2)}, u32[]{:S(2)}) async-start(bf16[8,80,1024]{2,1,0:T(8,128)(2,1)} %param.15), calls=%async_computation | async-start | bytes 2621440 | tf_op jit(solution)/shard_map/all_to_all | solution.py:160
  40.5 439.2 %reduce-scatter.9.cloned.1.call-start = ((), (), s32[]{:S(2)}) async-start(), calls=%async_computation.14 | async-start | bytes 8650752 | tf_op jit(solution)/shard_map/reduce_scatter | solution.py:113
  81.2 2.8 copy-start.2
  318.3 2.4 copy-start.24
  332.0 294.8 %reduce-scatter.11.cloned.1.call-start = ((), (), s32[]{:S(2)}) async-start(), calls=%async_computation.16 | async-start | bytes 8650752 | tf_op jit(solution)/shard_map/reduce_scatter | solution.py:113
  344.0 418.6 %reduce-scatter.7.cloned.1.call-start = ((), (), s32[]{:S(2)}) async-start(), calls=%async_computation.13 | async-start | bytes 2162688 | tf_op jit(solution)/shard_map/reduce_scatter | solution.py:113
  344.1 11.0 %copy-start.4 = (bf16[4,2,80,1024]{3,2,0,1:T(8,128)(2,1)S(1)}, bf16[4,2,80,1024]{3,2,0,1:T(8,128)(2,1)}, u32[]{:S(2)}) copy-start(bf16[4,2,80,1024]{3,2,0,1:T(8,128)(2,1)} %copy.36) | copy-start | bytes 3932164
  355.1 4.2 copy-start.9
  357.8 1.5 copy-start.5
  362.5 516.9 %reduce-scatter.5.cloned.1.call-start = ((), (), s32[]{:S(2)}) async-start(), calls=%async_computation.12 | async-start | bytes 6488064 | tf_op jit(solution)/shard_map/reduce_scatter | solution.py:113
  362.5 3.1 copy-start.6
  398.7 1.8 copy-start.12
  398.7 2.2 copy-start.11
  400.4 2.4 copy-start.10
  400.9 1.9 copy-start.7
  409.9 0.7 copy-start.14
  424.7 205.9 %all-to-all-start.1 = ((bf16[2,320,1024]{2,0,1:T(2,128)(2,1)}), bf16[2,320,1024]{2,0,1:T(2,128)(2,1)}, u32[]{:S(2)}, u32[]{:S(2)}) async-start(bf16[2,320,1024]{2,0,1:T(2,128)(2,1)} %copy.34), calls=%async_computation.1 | async-start | bytes 2621440 | tf_op jit(solution)/shard_map/all_to_all | solution.py:178
  429.1 467.9 %all-gather.17.cloned.1.call-start = ((), (), s32[]{:S(2)}) async-start(), calls=%async_computation.15 | async-start | bytes 1310720 | tf_op jit(solution)/shard_map/all_gather | solution.py:114
  429.4 3.3 copy-start.8
  479.7 435.4 %all-gather.19.cloned.1.call-start = ((), (), s32[]{:S(2)}) async-start(), calls=%async_computation.17 | async-start | bytes 1310720 | tf_op jit(solution)/shard_map/all_gather | solution.py:114
  630.6 60.5 %all-to-all-start.3 = ((bf16[2,320,1024]{2,0,1:T(2,128)(2,1)}), bf16[2,320,1024]{2,0,1:T(2,128)(2,1)S(1)}, u32[]{:S(2)}, u32[]{:S(2)}) async-start(bf16[2,320,1024]{2,0,1:T(2,128)(2,1)} %copy.37), calls=%async_computation.3 | async-start | bytes 2621440 | tf_op jit(solution)/shard_map/all_to_all | solution.py:204
  888.2 29.7 %copy-start.1 = (bf16[128,4096]{1,0:T(8,128)(2,1)S(1)}, bf16[128,4096]{1,0:T(8,128)(2,1)}, u32[]{:S(2)}) copy-start(bf16[128,4096]{1,0:T(8,128)(2,1)} %param.25) | copy-start | bytes 3145732
Sparse Core Ops, SparseCore 0:
  11.5 76.5 all-gather.8
  91.0 54.9 all-gather.10
  149.4 76.2 all-gather.12
  229.0 76.0 all-gather.14
  332.1 147.5 reduce-scatter.8
  481.9 144.9 reduce-scatter.10
  629.7 132.8 reduce-scatter.6
  769.1 110.1 reduce-scatter.4
  880.9 15.9 all-gather.16
  898.3 16.7 all-gather.18

commit v2 on v1

--- a/solution.py
+++ b/solution.py
@@ -5,6 +5,7 @@
 from jax import lax
 from jax.experimental import pallas as pl
 from jax.experimental.pallas import tpu as pltpu
+from jax.sharding import Mesh
 from jax.sharding import PartitionSpec as P
 
 HEAD_DIM = 64
@@ -12,7 +13,7 @@
 EPSILON = 1e-06
 BF16 = jnp.bfloat16
 F32 = jnp.float32
-ALL = ("fsdp", "seq")
+FSDP, SEQ = ("z", "y"), ("x", "c")
 
 
 def layer_stats(values):
@@ -59,7 +60,7 @@
     out_ref[0] = context.astype(BF16)
 
 
-def attend_back_kernel(len_ref, q_ref, k_ref, v_ref, g_ref, dq_ref, dk_ref, dv_ref):
+def attend_back_kernel(len_ref, q_ref, k_ref, v_ref, g_ref, out_ref):
     q, k, v, g = q_ref[0], k_ref[0], v_ref[0], g_ref[0]
     lane, key_ok = masks(len_ref[pl.program_id(0)], q.shape[0])
     dq, dk, dv = (jnp.zeros(q.shape, F32) for _ in range(3))
@@ -73,7 +74,10 @@
         dq = jnp.where(own, contract(grad_scores, k, 1, 0), dq)
         dk = jnp.where(own, contract(grad_scores, q, 0, 0), dk)
         dv = jnp.where(own, contract(probs.astype(BF16), g, 0, 0), dv)
-    dq_ref[0], dk_ref[0], dv_ref[0] = dq.astype(BF16), dk.astype(BF16), dv.astype(BF16)
+    width = out_ref.shape[2] // 3
+    for block, value in enumerate((dq, dk, dv)):
+        start = pl.multiple_of(block * width + pl.program_id(1) * LANES, LANES)
+        out_ref[0, :, pl.ds(start, LANES)] = value.astype(BF16)
 
 
 def attention(lengths, joint, grad_context=None):
@@ -82,7 +86,6 @@
     block = (1, slots, LANES)
     specs = [pl.BlockSpec(block, functools.partial(lambda b, i, h, n: (i, 0, b + h), b * pairs)) for b in range(3)]
     plain = pl.BlockSpec(block, lambda i, h, n: (i, 0, h))
-    shape = jax.ShapeDtypeStruct((images, slots, width), BF16)
     back = grad_context is not None
     flops = 2 * images * pairs * 2 * slots * slots * LANES * (5 if back else 2)
     return pl.pallas_call(
@@ -91,9 +94,9 @@
             num_scalar_prefetch=1,
             grid=(images, pairs),
             in_specs=specs + ([plain] if back else []),
-            out_specs=[plain] * 3 if back else plain,
+            out_specs=pl.BlockSpec((1, slots, 3 * width), lambda i, h, n: (i, 0, 0)) if back else plain,
         ),
-        out_shape=[shape] * 3 if back else shape,
+        out_shape=jax.ShapeDtypeStruct((images, slots, 3 * width if back else width), BF16),
         cost_estimate=pl.CostEstimate(
             flops=flops,
             bytes_accessed=images * slots * width * 2 * (7 if back else 4),
@@ -102,16 +105,276 @@
     )(lengths, joint, joint, joint, *([grad_context] if back else []))
 
 
-def gather_weight(weight):
-    parts = lax.axis_size("seq")
-    rows = weight.shape[0] // parts
-    mine = lax.dynamic_slice_in_dim(weight, lax.axis_index("seq") * rows, rows, 0)
-    return lax.all_gather(mine, ALL, axis=0, tiled=True)
-
-
-def scatter_grad(grad):
-    mine = lax.psum_scatter(grad, ALL, scatter_dimension=0, tiled=True)
-    return lax.all_gather(mine, "seq", axis=0, tiled=True).astype(F32)
+def swap(value, axis):
+    return lax.ppermute(value, axis, [(0, 1), (1, 0)])
+
+
+def exchange(blocks, axis):
+    return lax.all_to_all(blocks, axis, split_axis=0, concat_axis=0, tiled=True)
+
+
+def after(value, *others):
+    return lax.optimization_barrier((value,) + others)[0]
+
+
+def my_place():
+    return jnp.stack([lax.axis_index(n) for n in ("y", "x", "c")]).astype(jnp.int32)
+
+
+class Split:
+    def __init__(self, shard, by_rows):
+        self.shard_rows, self.columns = shard
+        self.by_rows = by_rows
+        self.rows = self.shard_rows // 4 if by_rows else self.shard_rows // 2
+        self.wide = self.columns if by_rows else self.columns // 2
+        self.via_y = self.rows * 3 // 4
+
+
+class Gather:
+    def __init__(self, weight, by_rows=False):
+        self.cut = Split(weight.shape, by_rows)
+        self.weight = weight
+
+    def over_z(self, *before):
+        cut = self.cut
+        x, c = lax.axis_index("x"), lax.axis_index("c")
+        at = (c * 2 * cut.rows + x * cut.rows, 0) if cut.by_rows else (x * cut.rows, c * cut.wide)
+        piece = lax.dynamic_slice(self.weight, at, (cut.rows, cut.wide))
+        if before:
+            piece = after(piece, *before)
+        depth = lax.axis_size("z")
+        self.z = exchange(jnp.broadcast_to(piece[None], (depth,) + piece.shape), "z")
+        return self.z
+
+    def over_plane(self, *before):
+        start = after(self.z, *before) if before else self.z
+        self.x, self.y = swap(start, "x"), swap(start, "y")
+        return self.x, self.y
+
+    def over_corner(self, *before):
+        x = after(self.x, *before) if before else self.x
+        cut = self.cut
+        self.d = (swap(x[:, : cut.via_y], "y"), swap(self.y[:, cut.via_y :], "x"))
+        return self.d
+
+    def whole(self):
+        cut = self.cut
+        mine = (self.z, self.x, self.y) + self.d
+        pieces = mine + tuple(swap(v, "c") for v in mine)
+        depth = self.z.shape[0]
+        return pl.pallas_call(
+            functools.partial(place_kernel, cut),
+            grid_spec=pltpu.PrefetchScalarGridSpec(
+                num_scalar_prefetch=1,
+                grid=(1,),
+                in_specs=[pl.BlockSpec(memory_space=pl.ANY)] * len(pieces),
+                out_specs=pl.BlockSpec(memory_space=pltpu.VMEM),
+                scratch_shapes=[pltpu.SemaphoreType.DMA],
+            ),
+            out_shape=jax.ShapeDtypeStruct((2 * depth * cut.shard_rows, cut.columns), BF16),
+            cost_estimate=pl.CostEstimate(
+                flops=0, bytes_accessed=8 * depth * cut.shard_rows * cut.columns, transcendentals=0
+            ),
+        )(my_place(), *pieces)
+
+
+def place_kernel(cut, place_ref, *refs):
+    *pieces, out_ref, sem = refs
+    y, x, c = place_ref[0], place_ref[1], place_ref[2]
+    copies = []
+    for core in range(2):
+        at, far_y, far_x, far_1, far_2 = pieces[5 * core : 5 * core + 5]
+        core_at = jnp.where(c == core, 0, 1)
+        for z in range(at.shape[0]):
+            for ref, other_y, other_x, off, rows in (
+                (at, 0, 0, 0, cut.rows),
+                (far_y, 0, 1, 0, cut.rows),
+                (far_x, 1, 0, 0, cut.rows),
+                (far_1, 1, 1, 0, cut.via_y),
+                (far_2, 1, 1, cut.via_y, cut.rows - cut.via_y),
+            ):
+                yy = jnp.where(y == other_y, 0, 1)
+                xx = jnp.where(x == other_x, 0, 1)
+                start = (2 * z + yy) * cut.shard_rows + xx * cut.rows + off
+                if cut.by_rows:
+                    start = start + core_at * 2 * cut.rows
+                rows_at = pl.ds(pl.multiple_of(start, 16), rows)
+                if cut.by_rows:
+                    target = out_ref.at[rows_at]
+                else:
+                    target = out_ref.at[rows_at, pl.ds(pl.multiple_of(core_at * cut.wide, 128), cut.wide)]
+                copies.append(pltpu.make_async_copy(ref.at[z], target, sem))
+    for copy in copies:
+        copy.start()
+    for copy in copies:
+        copy.wait()
+
+
+def parts_of(place_ref, by_y, rows, via_y, refs):
+    y, x = place_ref[0], place_ref[1]
+    near = jnp.where(y == 0, by_y[0], by_y[1]).astype(BF16)
+    far = jnp.where(y == 0, by_y[1], by_y[0]).astype(BF16)
+    own_ref, to_x_ref, to_y_ref, corner_1_ref, corner_2_ref = refs
+    low, high = near[:, :rows], near[:, rows:]
+    own_ref[...] = jnp.where(x == 0, low, high)
+    to_x_ref[...] = jnp.where(x == 0, high, low)
+    low, high = far[:, :rows], far[:, rows:]
+    to_y_ref[...] = jnp.where(x == 0, low, high)
+    corner = jnp.where(x == 0, high, low)
+    corner_1_ref[...] = corner[:, :via_y]
+    corner_2_ref[...] = corner[:, via_y:]
+
+
+def grad_columns_kernel(cut, place_ref, a_ref, a_sib_ref, g_ref, g_sib_ref, *out_refs):
+    total = contract(a_ref[...], g_ref[...], 0, 0) + contract(a_sib_ref[...], g_sib_ref[...], 0, 0)
+    total = total.reshape(-1, 2, cut.shard_rows, total.shape[1])
+    parts_of(place_ref, (total[:, 0], total[:, 1]), cut.rows, cut.via_y, out_refs)
+
+
+def grad_rows_kernel(cut, place_ref, a0_ref, a1_ref, a_sib_ref, g_ref, g_sib_ref, *out_refs):
+    half = 2 * cut.rows
+    by_y = [
+        (
+            contract(ref[...], g_ref[...], 0, 0)
+            + contract(a_sib_ref[:, yy * half : (yy + 1) * half], g_sib_ref[...], 0, 0)
+        )[None]
+        for yy, ref in enumerate((a0_ref, a1_ref))
+    ]
+    parts_of(place_ref, by_y, cut.rows, cut.via_y, out_refs)
+
+
+def grad_parts(cut, depth, a, a_sib, g, g_sib, step=512):
+    tokens = a.shape[0]
+    all_rows = lambda n: pl.BlockSpec((tokens, n), lambda j, place: (0, 0))
+    if cut.by_rows:
+        half = 2 * cut.rows
+        grid = (depth,)
+        in_specs = [
+            pl.BlockSpec((tokens, half), lambda j, place: (0, 4 * j + place[2])),
+            pl.BlockSpec((tokens, half), lambda j, place: (0, 4 * j + 2 + place[2])),
+            pl.BlockSpec((tokens, 2 * half), lambda j, place: (0, j)),
+            all_rows(cut.wide),
+            all_rows(cut.wide),
+        ]
+        out_spec = lambda rows: pl.BlockSpec((1, rows, cut.wide), lambda j, place: (j, 0, 0))
+        operands, kernel = (a, a, a_sib, g, g_sib), grad_rows_kernel
+    else:
+        steps = cut.wide // step
+        grid = (steps,)
+        in_specs = [
+            all_rows(a.shape[1]),
+            all_rows(a.shape[1]),
+            pl.BlockSpec((tokens, step), lambda j, place: (0, place[2] * steps + j)),
+            pl.BlockSpec((tokens, step), lambda j, place: (0, j)),
+        ]
+        out_spec = lambda rows: pl.BlockSpec((depth, rows, step), lambda j, place: (0, 0, j))
+        operands, kernel = (a, a_sib, g, g_sib), grad_columns_kernel
+    sizes = (cut.rows,) * 3 + (cut.via_y, cut.rows - cut.via_y)
+    total = 8 * depth * cut.rows * cut.wide
+    return pl.pallas_call(
+        functools.partial(kernel, cut),
+        grid_spec=pltpu.PrefetchScalarGridSpec(
+            num_scalar_prefetch=1,
+            grid=grid,
+            in_specs=in_specs,
+            out_specs=[out_spec(n) for n in sizes],
+        ),
+        out_shape=[jax.ShapeDtypeStruct((depth, n, cut.wide), BF16) for n in sizes],
+        compiler_params=pltpu.CompilerParams(vmem_limit_bytes=48 << 20),
+        cost_estimate=pl.CostEstimate(
+            flops=2 * total * tokens,
+            bytes_accessed=2 * total + sum(2 * v.size for v in (a, g)),
+            transcendentals=0,
+        ),
+    )(my_place(), *operands)
+
+
+class Scatter:
+    def __init__(self, cut, a, a_sib, g, g_sib):
+        self.cut = cut
+        depth = lax.axis_size("z")
+        self.own, self.to_x, self.to_y, self.c1, self.c2 = grad_parts(cut, depth, a, a_sib, g, g_sib)
+
+    def over_corner(self):
+        self.e1, self.e2 = swap(self.c1, "y"), swap(self.c2, "x")
+        return self.e1, self.e2
+
+    def over_plane(self):
+        n = self.cut.via_y
+        add = lambda u, v: (u.astype(F32) + v.astype(F32)).astype(BF16)
+        to_x = jnp.concatenate([add(self.to_x[:, :n], self.e1), self.to_x[:, n:]], axis=1)
+        to_y = jnp.concatenate([self.to_y[:, :n], add(self.to_y[:, n:], self.e2)], axis=1)
+        self.x, self.y = swap(to_x, "x"), swap(to_y, "y")
+        return self.x, self.y
+
+    def over_z(self):
+        total = sum(v.astype(F32) for v in (self.own, self.x, self.y)).astype(BF16)
+        self.z = exchange(total, "z")
+        return self.z
+
+    def whole(self):
+        x, c = lax.axis_index("x"), lax.axis_index("c")
+        mine = jnp.sum(self.z.astype(F32), axis=0).astype(BF16)
+        theirs = swap(mine, "x")
+        ours = jnp.concatenate(
+            [jnp.where(x == 0, mine, theirs), jnp.where(x == 0, theirs, mine)], axis=0
+        )
+        theirs = swap(ours, "c")
+        first, second = jnp.where(c == 0, ours, theirs), jnp.where(c == 0, theirs, ours)
+        return jnp.concatenate([first, second], axis=0 if self.cut.by_rows else 1).astype(F32)
+
+
+def for_sibling(value, groups):
+    half = value.shape[1] // groups // 2
+    first = lax.axis_index("c") == 0
+    cuts = [value[:, i * half : (i + 1) * half] for i in range(2 * groups)]
+    picked = [jnp.where(first, cuts[2 * i + 1], cuts[2 * i]) for i in range(groups)]
+    return swap(jnp.concatenate(picked, axis=1), "c")
+
+
+def gather_vectors(packed):
+    depth = lax.axis_size("z")
+    own_y = exchange(jnp.broadcast_to(packed[None], (depth,) + packed.shape), "z")
+    other_y = swap(own_y, "y")
+    y = lax.axis_index("y")
+    rows = [jnp.where(y == 0, own_y, other_y), jnp.where(y == 0, other_y, own_y)]
+    return jnp.stack(rows, axis=1).reshape(2 * depth, -1)
+
+
+def scatter_vectors(packed):
+    y = lax.axis_index("y")
+    packed = packed + swap(packed, "c")
+    packed = packed + swap(packed, "x")
+    packed = packed.reshape(lax.axis_size("z"), 2, -1)
+    row = lambda yy: lax.dynamic_slice_in_dim(packed, yy, 1, 1)[:, 0]
+    packed = row(y) + swap(row(1 - y), "y")
+    return jnp.sum(exchange(packed, "z"), axis=0)
+
+
+class Plain:
+    def __init__(self, a, g):
+        self.grad = contract(a, g, 0, 0).astype(BF16)
+
+    def whole(self):
+        grad = lax.psum_scatter(self.grad, FSDP, scatter_dimension=0, tiled=True)
+        return lax.psum(grad, SEQ).astype(F32)
+
+
+def gather_all(qkv, out, up, down):
+    qkv, out, up, down = Gather(qkv), Gather(out), Gather(up), Gather(down, by_rows=True)
+    first = qkv.over_z()
+    second = out.over_z(first)
+    plane = qkv.over_plane()
+    third = up.over_z(second, *plane)
+    corner = qkv.over_corner()
+    out_plane = out.over_plane(*plane)
+    down.over_z(third, *corner, *out_plane)
+    up_plane = up.over_plane(*corner, *out_plane)
+    out.over_corner()
+    down.over_plane(*up_plane)
+    up_corner = up.over_corner()
+    down.over_corner(*up_corner)
+    return [w.whole() for w in (qkv, out, up, down)]
 
 
 def shards(
@@ -132,33 +395,43 @@
     cotangent,
 ):
     width = tokens.shape[2]
-    members = lax.axis_size("seq")
+    members = lax.axis_size(SEQ)
+    staged = lax.axis_size("z") <= 8 and attn_weight.shape[0] % 128 == 0
     images = tokens.shape[0] // members
     slots = tokens.shape[1] * members
     rows = images * slots
 
     small = (attn_gain, attn_shift, attn_bias, out_bias, mlp_gain, mlp_shift, up_bias, down_bias)
     sizes = [v.shape[0] for v in small]
-    small_all = lax.all_gather(jnp.concatenate(small), "fsdp", axis=0).astype(F32)
+    small_all = gather_vectors(jnp.concatenate(small)).astype(F32)
     cuts = [sum(sizes[:i]) for i in range(len(sizes))]
     gain_a, shift_a, bias_qv, bias_out, gain_b, shift_b, bias_up, bias_down = (
         small_all[:, c : c + n].reshape(-1) for c, n in zip(cuts, sizes)
     )
-    qkv_full, out_full, up_full, down_full = (
-        gather_weight(w) for w in (attn_weight, out_weight, up_weight, down_weight)
-    )
-
-    lens = lax.dynamic_slice_in_dim(lengths, lax.axis_index("seq") * images, images, 0)
+    matrices = (attn_weight, out_weight, up_weight, down_weight)
+    if staged:
+        qkv_full, out_full, up_full, down_full = gather_all(*matrices)
+    else:
+        qkv_full, out_full, up_full, down_full = (
+            lax.all_gather(w, FSDP, axis=0, tiled=True) for w in matrices
+        )
+
+    lens = lax.dynamic_slice_in_dim(lengths, lax.axis_index(SEQ) * images, images, 0)
     valid = jnp.arange(slots, dtype=jnp.int32)[None, :] < lens[:, None]
     valid = valid.reshape(rows, 1)
-    by_image = functools.partial(
-        lax.all_to_all, axis_name="seq", split_axis=0, concat_axis=1, tiled=True
-    )
-    by_slot = functools.partial(
-        lax.all_to_all, axis_name="seq", split_axis=1, concat_axis=0, tiled=True
-    )
-    wide = by_image(tokens).reshape(rows, width).astype(F32)
-    cot = by_image(cotangent).reshape(rows, width)
+    few = tokens.shape[1]
+
+    def by_image(value):
+        value = exchange(value, SEQ).reshape(members, images, few, width)
+        return value.transpose(1, 0, 2, 3).reshape(rows, width)
+
+    def by_slot(value):
+        value = value.reshape(images, members, few, width).transpose(1, 0, 2, 3)
+        return exchange(value.reshape(members * images, few, width), SEQ)
+
+    tokens = by_image(tokens)
+    wide = tokens.astype(F32)
+    cot = by_image(after(cotangent, tokens))
 
     normal_a, inv_a = layer_stats(wide)
     normed_a = (normal_a * gain_a + shift_a).astype(BF16)
@@ -175,39 +448,69 @@
     slope = (cumul + pre * jnp.exp(-0.5 * pre * pre) * 0.3989422804014327).astype(BF16)
     result = middle + contract(hidden, down_full, 1, 0) + bias_down
     layer_out = jnp.where(valid, result, 0.0).astype(BF16)
-    layer_out = by_slot(layer_out.reshape(images, slots, width))
+    layer_out = by_slot(layer_out)
 
     grad_out = jnp.where(valid, cot, jnp.zeros_like(cot))
     grad_out_wide = grad_out.astype(F32)
+    shard_count = lax.axis_size(FSDP)
+
+    def scatter(weight, a, g, by_rows=False):
+        if not staged:
+            return Plain(a, g)
+        cut = Split(weight.shape, by_rows)
+        if by_rows:
+            return Scatter(cut, a, for_sibling(a, shard_count), g, swap(g, "c"))
+        return Scatter(cut, a, swap(a, "c"), g, for_sibling(g, 1))
+
     g_bias_down = jnp.sum(grad_out_wide, axis=0)
-    g_down = scatter_grad(contract(hidden, grad_out, 0, 0).astype(BF16))
+    s_down = scatter(down_weight, hidden, grad_out, by_rows=True)
     grad_pre = (contract(grad_out, down_full, 1, 1) * slope.astype(F32)).astype(BF16)
+    if staged:
+        grad_pre = after(grad_pre, *s_down.over_corner())
     g_bias_up = jnp.sum(grad_pre.astype(F32), axis=0)
-    g_up = scatter_grad(contract(normed_b, grad_pre, 0, 0).astype(BF16))
+    s_up = scatter(up_weight, normed_b, grad_pre)
     grad_nb = contract(grad_pre, up_full, 1, 1)
+    if staged:
+        grad_nb = after(grad_nb, s_up.own)
     g_gain_b = jnp.sum(grad_nb * normal_b, axis=0)
     g_shift_b = jnp.sum(grad_nb, axis=0)
     grad_middle = grad_out_wide + norm_back(grad_nb, gain_b, normal_b, inv_b)
     grad_branch = grad_middle.astype(BF16)
     g_bias_out = jnp.sum(grad_branch.astype(F32), axis=0)
-    g_out = scatter_grad(contract(context, grad_branch, 0, 0).astype(BF16))
+    s_out = scatter(out_weight, context, grad_branch)
     grad_context = contract(grad_branch, out_full, 1, 1).astype(BF16)
-    grad_parts = attention(lens, joint, grad_context.reshape(images, slots, width))
-    grad_joint = jnp.concatenate(grad_parts, axis=2).reshape(rows, 3 * width)
+    if staged:
+        s_up.over_corner()
+        s_out.over_corner()
+        grad_context = after(grad_context, *s_down.over_plane(), s_out.own)
+    grad_joint = attention(lens, joint, grad_context.reshape(images, slots, width))
+    grad_joint = grad_joint.reshape(rows, 3 * width)
+    if staged:
+        s_down.over_z()
+        s_up.over_plane()
+        s_out.over_plane()
+        grad_joint = after(grad_joint, s_up.e1, s_up.e2, s_out.e1, s_out.e2)
     joint_sums = jnp.sum(grad_joint.astype(F32), axis=0)
     g_bias_qv = jnp.concatenate([joint_sums[:width], joint_sums[2 * width :]])
-    g_qkv = scatter_grad(contract(normed_a, grad_joint, 0, 0).astype(BF16))
+    s_qkv = scatter(attn_weight, normed_a, grad_joint)
     grad_na = contract(grad_joint, qkv_full, 1, 1)
+    if staged:
+        s_qkv.over_corner()
+        grad_na = after(grad_na, s_up.x, s_up.y, s_out.x, s_out.y, s_down.z, s_qkv.own)
     g_gain_a = jnp.sum(grad_na * normal_a, axis=0)
     g_shift_a = jnp.sum(grad_na, axis=0)
     input_grad = (grad_middle + norm_back(grad_na, gain_a, normal_a, inv_a)).astype(BF16)
-    input_grad = by_slot(input_grad.reshape(images, slots, width))
-
-    shard_count = lax.axis_size("fsdp")
+    input_grad = by_slot(input_grad)
+    if staged:
+        s_up.over_z()
+        s_out.over_z()
+        s_qkv.over_plane()
+        s_qkv.over_z()
+    g_down, g_up, g_out, g_qkv = (v.whole() for v in (s_down, s_up, s_out, s_qkv))
+
     small_grads = (g_gain_a, g_shift_a, g_bias_qv, g_bias_out, g_gain_b, g_shift_b, g_bias_up, g_bias_down)
     packed = jnp.concatenate([v.reshape(shard_count, -1) for v in small_grads], axis=1)
-    packed = lax.psum(packed, ALL)
-    packed = lax.dynamic_slice_in_dim(packed, lax.axis_index("fsdp"), 1, 0)[0]
+    packed = scatter_vectors(packed)
     (g_gain_a, g_shift_a, g_bias_qv, g_bias_out, g_gain_b, g_shift_b, g_bias_up, g_bias_down) = (
         packed[c : c + n] for c, n in zip(cuts, sizes)
     )
@@ -230,11 +533,13 @@
 
 
 def solution(mesh):
-    rows, vector, matrix = P("fsdp", "seq", None), P("fsdp"), P("fsdp", None)
+    shard_count, members = mesh.devices.shape
+    fine = Mesh(mesh.devices.reshape(shard_count // 2, 2, members // 2, 2), FSDP + SEQ)
+    rows, vector, matrix = P(FSDP, SEQ, None), P(FSDP), P(FSDP, None)
     weights = (vector, vector, matrix, vector, matrix, vector, vector, vector, matrix, vector, matrix, vector)
     return jax.shard_map(
         shards,
-        mesh=mesh,
+        mesh=fine,
         in_specs=(rows, vector) + weights + (rows,),
         out_specs=(rows, rows) + weights,
         check_vma=False,

time: 932 us -> 635 us (0.68)
  waiting for transfers between devices: 573 us -> 206 us
  starting transfers between devices: 17.2 us -> 96.8 us
  blocking collectives: 98.9 us -> 26.2 us
  Pallas kernels: 48.4 us -> 107 us
  other arithmetic: 30.9 us -> 76.8 us
  matrix products: 109 us -> 68.3 us
  between operations: 15.1 us -> 2.7 us
    reduce_scatter x4 -> x0, waiting for transfers between devices: 361 us -> none  [scatter_grad(): mine = lax.psum_scatter(grad, ALL, scatter_dimension=0, tiled=True)]
    all_gather x6 -> x0, waiting for transfers between devices: 193 us -> none  [the longest x4 170 us: gather_weight(): return lax.all_gather(mine, ALL, axis=0, tiled=True)]
    ppermute x0 -> x72, waiting for transfers between devices: none -> 134 us  [swap(): return lax.ppermute(value, axis, [(0, 1), (1, 0)])]
    pallas_call x0 -> x8, Pallas kernels: none -> 57.9 us  [the longest x4 33.7 us: grad_parts(): pl.pallas_call(functools.partial(kernel, cut), grid_spec=pltpu.PrefetchSc...]
    all_to_all x4 -> x13, waiting for transfers between devices: 18.6 us -> 71.3 us  [exchange(): return lax.all_to_all(blocks, axis, split_axis=0, concat_axis=0, tiled=True)]
    psum x1 -> x0, blocking collectives: 52.2 us -> none  [shards(): packed = lax.psum(packed, ALL)]
    all_gather x3 -> x0, blocking collectives: 46.7 us -> none  [the longest x1 31.9 us: shards(): lax.all_gather(jnp.concatenate(small), 'fsdp', axis=0).astype(F32)]
    ppermute x0 -> x72, starting transfers between devices: none -> 44.3 us  [swap(): return lax.ppermute(value, axis, [(0, 1), (1, 0)])]
  transfers between devices with their start and end apart: 14 -> 85, of which waited for: 11 -> 30; matrix products, arithmetic and copies ran while one was open for 15% -> 27% of each run, Pallas kernels for 5% -> 17%
where the time goes in v2:
time: 635 us; the launch traced here: 625 us
  waiting for transfers between devices  206 us (32%)
  Pallas kernels  107 us (17%)
  starting transfers between devices  96.8 us (15%)
  other arithmetic  76.8 us (12%)
  matrix products  68.3 us (11%)
  local copies, waits for them, and re-layouts  41.5 us (7%)
  blocking collectives  26.2 us (4%)
    ppermute x72, waiting for transfers between devices, swap(): return lax.ppermute(value, axis, [(0, 1), (1, 0)])  134 us
    all_to_all x13, waiting for transfers between devices, exchange(): return lax.all_to_all(blocks, axis, split_axis=0, concat_axis=0, tiled=True)  71.3 us
    dot_general x8, matrix products, contract(): lax.dot_general(a, b, (((ca,), (cb,)), ((), ())), preferred_element_type=...  68.3 us
    all_to_all x13, starting transfers between devices, exchange(): return lax.all_to_all(blocks, axis, split_axis=0, concat_axis=0, tiled=True)  52.5 us
    pallas_call x2, Pallas kernels, attention(): pl.pallas_call(attend_back_kernel if back else attend_kernel, grid_spec=p...  48.8 us
    ppermute x72, starting transfers between devices, swap(): return lax.ppermute(value, axis, [(0, 1), (1, 0)])  44.3 us
    pallas_call x4, Pallas kernels, grad_parts(): pl.pallas_call(functools.partial(kernel, cut), grid_spec=pltpu.PrefetchSc...  33.7 us
    all_to_all x1, blocking collectives, exchange(): return lax.all_to_all(blocks, axis, split_axis=0, concat_axis=0, tiled=True)  26.2 us
  transfers between devices with their start and end apart: 85, of which 30 were waited for; matrix products, arithmetic and copies ran while one was open for 27% of the time, Pallas kernels for 17%

profile of v2, /device:TPU:0, one launch (start us, length us, event | category | flops | bytes accessed | tf_op | source)
XLA Modules:
  0.0 624.8 jit_solution(6374647446657910093)
XLA Ops:
  1.9 26.2 %all_to_all.78.refs_0_ = bf16[4,64,1536]{2,1,0:T(8,128)(2,1)S(1)} all-to-all(bf16[4,64,1536]{2,1,0:T(8,128)(2,1)S(1)} %broadcast_in_dim.31), channel_id=1, replica_groups=mesh['z'=4,'y'=2,'x'=2,'c'=2] {'z'}, dimensions={0} | all-to-all | bytes 1572864 | tf_op jit(solution)/shard_map/all_to_all | solution.py:113
  32.7 3.5 all-to-all-start.3
  39.9 3.3 all-to-all-done.3.refs_0_
  43.2 3.3 all-to-all-start.1
  47.6 4.4 all-to-all-done.1
  53.1 3.5 all-to-all-start.4
  61.3 17.1 %all-to-all-done.4.refs_0_ = bf16[4,64,2048]{2,1,0:T(8,128)(2,1)S(1)} async-done(((bf16[4,64,2048]{2,1,0:T(8,128)(2,1)}), bf16[4,64,2048]{2,1,0:T(8,128)(2,1)S(1)}, u32[]{:S(2)}, u32[]{:S(2)}) %all-to-all-start.4) | async-done | bytes 1048608 | tf_op jit(solution)/shard_map/all_to_all | solution.py:113
  79.4 3.5 all-to-all-start
  89.4 20.6 %collective-permute-done.4.refs_4_ = bf16[4,16,1536]{2,1,0:T(8,128)(2,1)S(1)} collective-permute-done((bf16[4,16,1536]{2,1,0:T(8,128)(2,1)S(1)}, bf16[4,16,1536]{2,1,0:T(8,128)(2,1)S(1)}, u32[]{:S(2)}, u32[]{:S(2)}) %collective-permute-start.4) | collective-permute-done | bytes 196640 | tf_op jit(solution)/shard_map/ppermute | solution.py:109
  112.9 2.7 collective-permute-done.13.refs_4_
  119.8 3.4 collective-permute-done.17.refs_8_
  125.0 4.3 all-to-all-start.5
  130.6 3.6 shard_map.256
  135.0 6.2 shard_map.254
  147.3 8.5 %add_convert_fusion = bf16[640,3072]{1,0:T(8,128)(2,1)} fusion(bf16[640,1024]{1,0:T(8,128)(2,1)S(1)} %fusion.11.a_ref, bf16[1024,3072]{1,0:T(8,128)(2,1)} %shard_map.254, f32[3072]{0:T(1024)S(1)} %copy-done.72), kind=kOutput, calls=%fused_computation.11 | convolution fusion | flops 4030464000 | bytes 11546624 | tf_op jit(solution)/shard_map/dot_general | solution.py:35
  155.8 19.2 %shard_map.255 = bf16[2,320,1024]{2,1,0:T(8,128)(2,1)} custom-call(s32[2]{0:T(128)} %dynamic_slice.21.len_ref, bf16[2,320,3072]{2,1,0:T(8,128)(2,1)} %bitcast.101, bf16[2,320,3072]{2,1,0:T(8,128)(2,1)} %bitcast.102, bf16[2,320,3072]{2,1,0:T(8,128)(2,1)} %bitcast.103), custom_call_target="tpu_custom_call" | custom-call | flops 1677721600 | bytes 5242880 | tf_op jit(solution)/shard_map/pallas_call | solution.py:91
  175.5 4.8 all-to-all-start.7
  182.5 3.6 fusion.30
  186.6 33.6 %collective-permute-done.28.refs_1_ = bf16[4,128,1024]{2,1,0:T(8,128)(2,1)} collective-permute-done((bf16[4,128,1024]{2,1,0:T(8,128)(2,1)}, bf16[4,128,1024]{2,1,0:T(8,128)(2,1)}, u32[]{:S(2)}, u32[]{:S(2)}) %collective-permute-start.28) | collective-permute-done | bytes 1048608 | tf_op jit(solution)/shard_map/ppermute | solution.py:109
  226.5 7.2 %shard_map.257 = bf16[1024,4096]{1,0:T(8,128)(2,1)} custom-call(s32[3]{0:T(128)} %pad_add_fusion.place_ref, bf16[4,64,2048]{2,1,0:T(8,128)(2,1)} %copy-done.32, bf16[4,64,2048]{2,1,0:T(8,128)(2,1)} %collective-permute-done.19.refs_1_, bf16[4,64,2048]{2,1,0:T(8,128)(2,1)} %collective-permute-done.20.refs_2_, ...), custom_call_target="tpu_custom_call" | custom-call | bytes 16777216 | tf_op jit(solution)/shard_map/pallas_call | solution.py:165
  233.8 11.5 %multiply_convert_fusion.1 = (bf16[640,4096]{1,0:T(8,128)(2,1)S(1)}, f32[640,4096]{1,0:T(8,128)}) fusion(f32[4096]{0:T(1024)S(1)} %bitcast.121, bf16[640,1024]{1,0:T(8,128)(2,1)} %add_convert_fusion.1.a_ref, bf16[1024,4096]{1,0:T(8,128)(2,1)} %shard_map.257), kind=kOutput, calls=%fused_computation.8 | convolution fusion | flops 5384437760 | bytes 25444352 | tf_op jit(solution)/shard_map/dot_general | solution.py:35
  253.3 13.1 %collective-permute-done.30.refs_3_ = bf16[4,96,1024]{2,1,0:T(8,128)(2,1)S(1)} collective-permute-done((bf16[4,96,1024]{2,1,0:T(8,128)(2,1)}, bf16[4,96,1024]{2,1,0:T(8,128)(2,1)S(1)}, u32[]{:S(2)}, u32[]{:S(2)}) %collective-permute-start.30) | collective-permute-done | bytes 786464 | tf_op jit(solution)/shard_map/ppermute | solution.py:109
  270.3 6.9 %collective-permute-done.31.refs_4_ = bf16[4,32,1024]{2,1,0:T(8,128)(2,1)} collective-permute-done((bf16[4,32,1024]{2,1,0:T(8,128)(2,1)}, bf16[4,32,1024]{2,1,0:T(8,128)(2,1)}, u32[]{:S(2)}, u32[]{:S(2)}) %collective-permute-start.31) | collective-permute-done | bytes 262176 | tf_op jit(solution)/shard_map/ppermute | solution.py:109
  279.7 7.3 %shard_map.258 = bf16[4096,1024]{1,0:T(8,128)(2,1)} custom-call(s32[3]{0:T(128)} %pad_add_fusion.place_ref, bf16[4,128,1024]{2,1,0:T(8,128)(2,1)} %all-to-all-done.5.refs_0_, bf16[4,128,1024]{2,1,0:T(8,128)(2,1)} %collective-permute-done.28.refs_1_, bf16[4,128,1024]{2,1,0:T(8,128)(2,1)} %collective-permute-done.29.refs_2_, bf16[4,96,1024]{2,1,0:T(8,128)(2,1)} %copy-done.47, ...), custom_call_target="tpu_custom_call" | custom-call | bytes 16777216 | tf_op jit(solution)/shard_map/pallas_call | solution.py:165
  287.0 10.0 %select_convert_fusion = bf16[640,1024]{1,0:T(8,128)(2,1)S(1)} fusion(f32[640,1024]{1,0:T(8,128)} %copy-done.19, bf16[640,4096]{1,0:T(8,128)(2,1)} %copy-done.31, bf16[4096,1024]{1,0:T(8,128)(2,1)} %shard_map.258, f32[1024]{0:T(1024)S(1)} %copy-done.74, pred[640]{0:T(1024)(128)(4,1)S(1)} %lt.65), kind=kOutput, calls=%fused_computation.37 | convolution fusion | flops 5371330560 | bytes 17568384 | tf_op jit(solution)/shard_map/dot_general | solution.py:35
  298.2 4.5 all-to-all-start.6
  302.7 10.4 %shard_map.259 = (bf16[4,128,1024]{2,1,0:T(8,128)(2,1)S(1)}, bf16[4,128,1024]{2,1,0:T(8,128)(2,1)S(1)}, bf16[4,128,1024]{2,1,0:T(8,128)(2,1)S(1)}, bf16[4,96,102...) custom-call(s32[3]{0:T(128)S(1)} %copy-done.12, bf16[640,4096]{1,0:T(8,128)(2,1)} %copy-done.31, bf16[640,4096]{1,0:T(8,128)(2,1)} %copy-done.31, ...), custom_call_target="tpu_custom_call" | custom-call | flops 5368709120 | bytes 14942208 | tf_op jit(solution)/shard_map/pallas_call | solution.py:274
  316.0 12.8 %multiply_convert_fusion.g_ref = bf16[640,4096]{1,0:T(8,128)(2,1)S(1)} fusion(bf16[640,1024]{1,0:T(8,128)(2,1)} %bitcast_select_fusion.g_ref, bf16[4096,1024]{1,0:T(8,128)(2,1)} %shard_map.258, f32[640,4096]{1,0:T(8,128)} %get-tuple-element.130, f32[4096]{0:T(1024)S(1)} %bitcast.122), kind=kOutput, calls=%fused_computation.7 | convolution fusion | flops 5402787840 | bytes 25444352 | tf_op jit(solution)/shard_map/dot_general | solution.py:35
  339.3 2.2 convert_reduce_fusion.3
  341.6 3.6 convert_reduce_fusion
  345.8 9.9 %collective-permute-done.44 = bf16[4,128,1024]{2,1,0:T(8,128)(2,1)} collective-permute-done((bf16[4,128,1024]{2,1,0:T(8,128)(2,1)}, bf16[4,128,1024]{2,1,0:T(8,128)(2,1)}, u32[]{:S(2)}, u32[]{:S(2)}) %collective-permute-start.44) | collective-permute-done | bytes 1048608 | tf_op jit(solution)/shard_map/ppermute | solution.py:109
  355.7 3.9 collective-permute-done.43
  359.5 3.5 add_convert_fusion.3
  363.0 5.3 all-to-all-start.8
  368.3 10.7 %fusion.31 = f32[640,1024]{1,0:T(8,128)} fusion(bf16[640,4096]{1,0:T(8,128)(2,1)} %copy-done.25, bf16[1024,4096]{1,0:T(8,128)(2,1)} %shard_map.257), kind=kOutput, calls=%fused_computation.149 | convolution fusion | flops 5368709120 | bytes 16252928 | tf_op jit(solution)/shard_map/dot_general | solution.py:35
  379.0 13.6 %all-to-all-done.8 = bf16[4,128,1024]{2,1,0:T(8,128)(2,1)} async-done(((bf16[4,128,1024]{2,1,0:T(8,128)(2,1)}), bf16[4,128,1024]{2,1,0:T(8,128)(2,1)}, u32[]{:S(2)}, u32[]{:S(2)}) %all-to-all-start.8) | async-done | bytes 1048608 | tf_op jit(solution)/shard_map/all_to_all | solution.py:113
  395.4 11.2 %shard_map.260 = (bf16[4,64,2048]{2,1,0:T(8,128)(2,1)S(1)}, bf16[4,64,2048]{2,1,0:T(8,128)(2,1)S(1)}, bf16[4,64,2048]{2,1,0:T(8,128)(2,1)S(1)}, bf16[4,48,2048]{2,1,0:T(8,128)(2,1)}, bf16[4,16,2048]{2,1,0:T(8,128)(2,1)S(1)}) custom-call(s32[3]{0:T(128)S(1)} %copy-done.12, bf16[640,1024]{1,0:T(8,128)(2,1)} %add_convert_fusion.1.a_ref, ...), custom_call_target="tpu_custom_call" | custom-call | flops 5368709120 | bytes 14942208 | tf_op jit(solution)/shard_map/pallas_call | solution.py:274
  406.6 4.2 multiply_reduce_fusion
  410.8 3.0 convert_reduce_fusion.4
  415.4 2.6 convolution_convert_fusion
  421.4 5.0 collective-permute-done.48
  428.9 3.7 shard_map.261
  434.8 29.6 %shard_map.262 = bf16[2,320,3072]{2,1,0:T(8,128)(2,1)} custom-call(s32[2]{0:T(128)} %dynamic_slice.21.len_ref, bf16[2,320,3072]{2,1,0:T(8,128)(2,1)} %bitcast.104, bf16[2,320,3072]{2,1,0:T(8,128)(2,1)} %bitcast.105, bf16[2,320,3072]{2,1,0:T(8,128)(2,1)} %bitcast.106, bf16[2,320,1024]{2,1,0:T(8,128)(2,1)} %bitcast.118), custom_call_target="tpu_custom_call" | custom-call | flops 4194304000 | bytes 9175040 | tf_op jit(solution)/shard_map/pallas_call | solution.py:91
  468.8 3.5 collective-permute-done.49
  473.8 8.7 %fusion.32 = f32[640,1024]{1,0:T(8,128)} fusion(bf16[640,3072]{1,0:T(8,128)(2,1)S(1)} %bitcast.109, bf16[1024,3072]{1,0:T(8,128)(2,1)} %shard_map.254), kind=kOutput, calls=%fused_computation.150 | convolution fusion | flops 4026531840 | bytes 12845056 | tf_op jit(solution)/shard_map/dot_general | solution.py:35
  484.2 13.1 %collective-permute-done.53 = bf16[4,64,512]{2,1,0:T(8,128)(2,1)S(1)} collective-permute-done((bf16[4,64,512]{2,1,0:T(8,128)(2,1)S(1)}, bf16[4,64,512]{2,1,0:T(8,128)(2,1)S(1)}, u32[]{:S(2)}, u32[]{:S(2)}) %collective-permute-start.53) | collective-permute-done | bytes 262176 | tf_op jit(solution)/shard_map/ppermute | solution.py:109
  499.0 4.0 all-to-all-start.12
  503.1 8.4 %shard_map.263 = (bf16[4,64,1536]{2,1,0:T(8,128)(2,1)S(1)}, bf16[4,64,1536]{2,1,0:T(8,128)(2,1)S(1)}, bf16[4,64,1536]{2,1,0:T(8,128)(2,1)S(1)}, bf16[4,48,1536]{2,1,0:T(8,128)(2,1)S(1)}, bf16[4,16,1536]{2,1,0:T(8,128)(2,1)S(1)}) custom-call(s32[3]{0:T(128)S(1)} %copy-done.12, bf16[640,1024]{1,0:T(8,128)(2,1)S(1)} %fusion.11.a_ref, ...), custom_call_target="tpu_custom_call" | custom-call | flops 4026531840 | bytes 11534336 | tf_op jit(solution)/shard_map/pallas_call | solution.py:274
  514.6 2.3 broadcast_select_fusion.1
  520.2 3.1 add_convert_fusion.2
  527.9 4.9 all-to-all-start.10
  535.0 3.4 all-to-all-done.10
  539.0 3.5 all-to-all-start.13
  546.5 3.3 collective-permute-done.60
  553.5 2.4 fusion.16
  557.1 8.6 %all-to-all-done.13 = bf16[4,64,2048]{2,1,0:T(8,128)(2,1)S(1)} async-done(((bf16[4,64,2048]{2,1,0:T(8,128)(2,1)}), bf16[4,64,2048]{2,1,0:T(8,128)(2,1)S(1)}, u32[]{:S(2)}, u32[]{:S(2)}) %all-to-all-start.13) | async-done | bytes 1048608 | tf_op jit(solution)/shard_map/all_to_all | solution.py:113
  566.6 3.8 all-to-all-start.9
  570.5 2.9 maximum_convert_fusion.1
  577.4 2.6 add_convert_fusion.4
  580.0 8.2 %all-to-all-done.9 = bf16[8,80,1024]{2,1,0:T(8,128)(2,1)S(1)} async-done(((bf16[8,80,1024]{2,1,0:T(8,128)(2,1)}), bf16[8,80,1024]{2,1,0:T(8,128)(2,1)S(1)}, u32[]{:S(2)}, u32[]{:S(2)}) %all-to-all-start.9) | async-done | bytes 1310752 | tf_op jit(solution)/shard_map/all_to_all | solution.py:113
  588.2 3.5 all-to-all-start.11
  598.7 12.7 %all-to-all-done.11 = bf16[4,64,1536]{2,1,0:T(8,128)(2,1)S(1)} async-done(((bf16[4,64,1536]{2,1,0:T(8,128)(2,1)}), bf16[4,64,1536]{2,1,0:T(8,128)(2,1)S(1)}, u32[]{:S(2)}, u32[]{:S(2)}) %all-to-all-start.11) | async-done | bytes 786464 | tf_op jit(solution)/shard_map/all_to_all | solution.py:113
  612.4 5.0 collective-permute-done.64
  620.7 2.6 copy.93
  (453 shorter events, 140.9 us)
Async XLA Ops:
  28.1 19.3 %collective-permute-start.1 = (bf16[4,64,1536]{2,1,0:T(8,128)(2,1)S(1)}, bf16[4,64,1536]{2,1,0:T(8,128)(2,1)}, u32[]{:S(2)}, u32[]{:S(2)}) collective-permute-start(bf16[4,64,1536]{2,1,0:T(8,128)(2,1)S(1)} %all_to_all.78.refs_0_), channel_id=1, source_target_pairs={{0,2},{2,0},{1,3},{3,1},{4,6},{6,4},{5,7},{7,5},{8,10},{10,8},{9,1... | collective-permute-start | bytes 2359304 | tf_op jit(solution)/shard_map/ppermute | solution.py:109
  29.6 18.0 %collective-permute-start.2 = (bf16[4,64,1536]{2,1,0:T(8,128)(2,1)S(1)}, bf16[4,64,1536]{2,1,0:T(8,128)(2,1)}, u32[]{:S(2)}, u32[]{:S(2)}) collective-permute-start(bf16[4,64,1536]{2,1,0:T(8,128)(2,1)S(1)} %all_to_all.78.refs_0_), channel_id=1, source_target_pairs={{0,4},{4,0},{1,5},{5,1},{2,6},{6,2},{3,7},{7,3},{8,12},{12,8},{9,1... | collective-permute-start | bytes 2359304 | tf_op jit(solution)/shard_map/ppermute | solution.py:109
  53.1 25.3 %all-to-all-start.4 = ((bf16[4,64,2048]{2,1,0:T(8,128)(2,1)}), bf16[4,64,2048]{2,1,0:T(8,128)(2,1)S(1)}, u32[]{:S(2)}, u32[]{:S(2)}) async-start(bf16[4,64,2048]{2,1,0:T(8,128)(2,1)} %broadcast_in_dim.38), calls=%async_computation.4 | async-start | bytes 2097152 | tf_op jit(solution)/shard_map/all_to_all | solution.py:113
  61.2 51.7 %collective-permute-start.5 = (bf16[4,64,1536]{2,1,0:T(8,128)(2,1)S(1)}, bf16[4,64,1536]{2,1,0:T(8,128)(2,1)}, u32[]{:S(2)}, u32[]{:S(2)}) collective-permute-start(bf16[4,64,1536]{2,1,0:T(8,128)(2,1)S(1)} %all_to_all.78.refs_0_), channel_id=1, source_target_pairs={{0,1},{1,0},{2,3},{3,2},{4,5},{5,4},{6,7},{7,6},{8,9},{9,8},{10,11... | collective-permute-start | bytes 2359304 | tf_op jit(solution)/shard_map/ppermute | solution.py:109
  79.4 39.4 %all-to-all-start = ((bf16[8,80,1024]{2,1,0:T(8,128)(2,1)}), bf16[8,80,1024]{2,1,0:T(8,128)(2,1)S(1)}, u32[]{:S(2)}, u32[]{:S(2)}) async-start(bf16[8,80,1024]{2,1,0:T(8,128)(2,1)} %param.15), calls=%async_computation | async-start | bytes 2621440 | tf_op jit(solution)/shard_map/all_to_all | solution.py:113
  83.1 28.1 %collective-permute-start.10 = (bf16[4,64,512]{2,1,0:T(8,128)(2,1)S(1)}, bf16[4,64,512]{2,1,0:T(8,128)(2,1)S(1)}, u32[]{:S(2)}, u32[]{:S(2)}) collective-permute-start(bf16[4,64,512]{2,1,0:T(8,128)(2,1)S(1)} %copy-done.43), channel_id=1, source_target_pairs={{0,2},{2,0},{1,3},{3,1},{4,6},{6,4},{5,7},{7,5},{8,10},{10,8},{9,1... | collective-permute-start | bytes 786440 | tf_op jit(solution)/shard_map/ppermute | solution.py:109
  85.1 25.6 %collective-permute-start.11 = (bf16[4,64,512]{2,1,0:T(8,128)(2,1)S(1)}, bf16[4,64,512]{2,1,0:T(8,128)(2,1)S(1)}, u32[]{:S(2)}, u32[]{:S(2)}) collective-permute-start(bf16[4,64,512]{2,1,0:T(8,128)(2,1)S(1)} %copy-done.43), channel_id=1, source_target_pairs={{0,4},{4,0},{1,5},{5,1},{2,6},{6,2},{3,7},{7,3},{8,12},{12,8},{9,1... | collective-permute-start | bytes 786440 | tf_op jit(solution)/shard_map/ppermute | solution.py:109
  86.7 28.8 %collective-permute-start.3 = (bf16[4,48,1536]{2,1,0:T(8,128)(2,1)S(1)}, bf16[4,48,1536]{2,1,0:T(8,128)(2,1)S(1)}, u32[]{:S(2)}, u32[]{:S(2)}) collective-permute-start(bf16[4,48,1536]{2,1,0:T(8,128)(2,1)S(1)} %slice.295), channel_id=1, source_target_pairs={{0,4},{4,0},{1,5},{5,1},{2,6},{6,2},{3,7},{7,3},{8,12},{12,8},{9,1... | collective-permute-start | bytes 1769480 | tf_op jit(solution)/shard_map/ppermute | solution.py:109
  89.2 20.8 %collective-permute-start.4 = (bf16[4,16,1536]{2,1,0:T(8,128)(2,1)S(1)}, bf16[4,16,1536]{2,1,0:T(8,128)(2,1)S(1)}, u32[]{:S(2)}, u32[]{:S(2)}) collective-permute-start(bf16[4,16,1536]{2,1,0:T(8,128)(2,1)S(1)} %slice.296), channel_id=1, source_target_pairs={{0,2},{2,0},{1,3},{3,1},{4,6},{6,4},{5,7},{7,5},{8,10},{10,8},{9,1... | collective-permute-start | bytes 589832 | tf_op jit(solution)/shard_map/ppermute | solution.py:109
  117.3 25.6 %collective-permute-start.19 = (bf16[4,64,2048]{2,1,0:T(8,128)(2,1)}, bf16[4,64,2048]{2,1,0:T(8,128)(2,1)}, u32[]{:S(2)}, u32[]{:S(2)}) collective-permute-start(bf16[4,64,2048]{2,1,0:T(8,128)(2,1)} %copy-done.32), channel_id=1, source_target_pairs={{0,2},{2,0},{1,3},{3,1},{4,6},{6,4},{5,7},{7,5},{8,10},{10,8},{9,1... | collective-permute-start | bytes 3145736 | tf_op jit(solution)/shard_map/ppermute | solution.py:109
  118.3 26.3 %collective-permute-start.20 = (bf16[4,64,2048]{2,1,0:T(8,128)(2,1)}, bf16[4,64,2048]{2,1,0:T(8,128)(2,1)}, u32[]{:S(2)}, u32[]{:S(2)}) collective-permute-start(bf16[4,64,2048]{2,1,0:T(8,128)(2,1)} %copy-done.32), channel_id=1, source_target_pairs={{0,4},{4,0},{1,5},{5,1},{2,6},{6,2},{3,7},{7,3},{8,12},{12,8},{9,1... | collective-permute-start | bytes 3145736 | tf_op jit(solution)/shard_map/ppermute | solution.py:109
  119.2 14.9 %collective-permute-start.6 = (bf16[4,64,1536]{2,1,0:T(8,128)(2,1)}, bf16[4,64,1536]{2,1,0:T(8,128)(2,1)S(1)}, u32[]{:S(2)}, u32[]{:S(2)}) collective-permute-start(bf16[4,64,1536]{2,1,0:T(8,128)(2,1)} %collective-permute-done.1.refs_1_), channel_id=1, source_target_pairs={{0,1},{1,0},{2,3},{3,2},{4,5},{5,4},{6,7},{7,6},{8,9},{9,8},{10,11... | collective-permute-start | bytes 2359304 | tf_op jit(solution)/shard_map/ppermute | solution.py:109
  119.2 14.9 %collective-permute-start.7 = (bf16[4,64,1536]{2,1,0:T(8,128)(2,1)}, bf16[4,64,1536]{2,1,0:T(8,128)(2,1)}, u32[]{:S(2)}, u32[]{:S(2)}) collective-permute-start(bf16[4,64,1536]{2,1,0:T(8,128)(2,1)} %collective-permute-done.2.refs_2_), channel_id=1, source_target_pairs={{0,1},{1,0},{2,3},{3,2},{4,5},{5,4},{6,7},{7,6},{8,9},{9,8},{10,11... | collective-permute-start | bytes 2359304 | tf_op jit(solution)/shard_map/ppermute | solution.py:109
  123.3 10.9 %collective-permute-start.8 = (bf16[4,48,1536]{2,1,0:T(8,128)(2,1)}, bf16[4,48,1536]{2,1,0:T(8,128)(2,1)}, u32[]{:S(2)}, u32[]{:S(2)}) collective-permute-start(bf16[4,48,1536]{2,1,0:T(8,128)(2,1)} %copy-done.49), channel_id=1, source_target_pairs={{0,1},{1,0},{2,3},{3,2},{4,5},{5,4},{6,7},{7,6},{8,9},{9,8},{10,11... | collective-permute-start | bytes 1769480 | tf_op jit(solution)/shard_map/ppermute | solution.py:109
  125.0 50.5 %all-to-all-start.5 = ((bf16[4,128,1024]{2,1,0:T(8,128)(2,1)}), bf16[4,128,1024]{2,1,0:T(8,128)(2,1)}, u32[]{:S(2)}, u32[]{:S(2)}) async-start(bf16[4,128,1024]{2,1,0:T(8,128)(2,1)} %broadcast_in_dim.39), calls=%async_computation.5 | async-start | bytes 2097152 | tf_op jit(solution)/shard_map/all_to_all | solution.py:113
  144.0 42.0 %collective-permute-start.21 = (bf16[4,48,2048]{2,1,0:T(8,128)(2,1)S(1)}, bf16[4,48,2048]{2,1,0:T(8,128)(2,1)}, u32[]{:S(2)}, u32[]{:S(2)}) collective-permute-start(bf16[4,48,2048]{2,1,0:T(8,128)(2,1)S(1)} %slice.304), channel_id=1, source_target_pairs={{0,4},{4,0},{1,5},{5,1},{2,6},{6,2},{3,7},{7,3},{8,12},{12,8},{9,1... | collective-permute-start | bytes 2359304 | tf_op jit(solution)/shard_map/ppermute | solution.py:109
  146.3 34.1 %collective-permute-start.22 = (bf16[4,16,2048]{2,1,0:T(8,128)(2,1)}, bf16[4,16,2048]{2,1,0:T(8,128)(2,1)}, u32[]{:S(2)}, u32[]{:S(2)}) collective-permute-start(bf16[4,16,2048]{2,1,0:T(8,128)(2,1)} %slice.305), channel_id=1, source_target_pairs={{0,2},{2,0},{1,3},{3,1},{4,6},{6,4},{5,7},{7,5},{8,10},{10,8},{9,1... | collective-permute-start | bytes 786440 | tf_op jit(solution)/shard_map/ppermute | solution.py:109
  175.0 48.8 %collective-permute-start.23 = (bf16[4,64,2048]{2,1,0:T(8,128)(2,1)}, bf16[4,64,2048]{2,1,0:T(8,128)(2,1)}, u32[]{:S(2)}, u32[]{:S(2)}) collective-permute-start(bf16[4,64,2048]{2,1,0:T(8,128)(2,1)} %copy-done.32), channel_id=1, source_target_pairs={{0,1},{1,0},{2,3},{3,2},{4,5},{5,4},{6,7},{7,6},{8,9},{9,8},{10,11... | collective-permute-start | bytes 3145736 | tf_op jit(solution)/shard_map/ppermute | solution.py:109
  175.0 50.4 %collective-permute-start.24 = (bf16[4,64,2048]{2,1,0:T(8,128)(2,1)}, bf16[4,64,2048]{2,1,0:T(8,128)(2,1)}, u32[]{:S(2)}, u32[]{:S(2)}) collective-permute-start(bf16[4,64,2048]{2,1,0:T(8,128)(2,1)} %collective-permute-done.19.refs_1_), channel_id=1, source_target_pairs={{0,1},{1,0},{2,3},{3,2},{4,5},{5,4},{6,7},{7,6},{8,9},{9,8},{10,11... | collective-permute-start | bytes 3145736 | tf_op jit(solution)/shard_map/ppermute | solution.py:109
  175.5 51.1 %collective-permute-start.25 = (bf16[4,64,2048]{2,1,0:T(8,128)(2,1)}, bf16[4,64,2048]{2,1,0:T(8,128)(2,1)}, u32[]{:S(2)}, u32[]{:S(2)}) collective-permute-start(bf16[4,64,2048]{2,1,0:T(8,128)(2,1)} %collective-permute-done.20.refs_2_), channel_id=1, source_target_pairs={{0,1},{1,0},{2,3},{3,2},{4,5},{5,4},{6,7},{7,6},{8,9},{9,8},{10,11... | collective-permute-start | bytes 3145736 | tf_op jit(solution)/shard_map/ppermute | solution.py:109
  175.5 93.3 %all-to-all-start.7 = ((bf16[8,80,1024]{2,1,0:T(8,128)(2,1)}), bf16[8,80,1024]{2,1,0:T(8,128)(2,1)}, u32[]{:S(2)}, u32[]{:S(2)}) async-start(bf16[8,80,1024]{2,1,0:T(8,128)(2,1)} %param.29), calls=%async_computation.7 | async-start | bytes 2621440 | tf_op jit(solution)/shard_map/all_to_all | solution.py:113
  180.4 39.8 %collective-permute-start.28 = (bf16[4,128,1024]{2,1,0:T(8,128)(2,1)}, bf16[4,128,1024]{2,1,0:T(8,128)(2,1)}, u32[]{:S(2)}, u32[]{:S(2)}) collective-permute-start(bf16[4,128,1024]{2,1,0:T(8,128)(2,1)} %all-to-all-done.5.refs_0_), channel_id=1, source_target_pairs={{0,2},{2,0},{1,3},{3,1},{4,6},{6,4},{5,7},{7,5},{8,10},{10,8},{9,1... | collective-permute-start | bytes 3145736 | tf_op jit(solution)/shard_map/ppermute | solution.py:109
  186.1 40.5 %collective-permute-start.26 = (bf16[4,48,2048]{2,1,0:T(8,128)(2,1)}, bf16[4,48,2048]{2,1,0:T(8,128)(2,1)}, u32[]{:S(2)}, u32[]{:S(2)}) collective-permute-start(bf16[4,48,2048]{2,1,0:T(8,128)(2,1)} %collective-permute-done.21.refs_3_), channel_id=1, source_target_pairs={{0,1},{1,0},{2,3},{3,2},{4,5},{5,4},{6,7},{7,6},{8,9},{9,8},{10,11... | collective-permute-start | bytes 2359304 | tf_op jit(solution)/shard_map/ppermute | solution.py:109
  223.8 28.1 %collective-permute-start.29 = (bf16[4,128,1024]{2,1,0:T(8,128)(2,1)}, bf16[4,128,1024]{2,1,0:T(8,128)(2,1)}, u32[]{:S(2)}, u32[]{:S(2)}) collective-permute-start(bf16[4,128,1024]{2,1,0:T(8,128)(2,1)} %all-to-all-done.5.refs_0_), channel_id=1, source_target_pairs={{0,4},{4,0},{1,5},{5,1},{2,6},{6,2},{3,7},{7,3},{8,12},{12,8},{9,1... | collective-permute-start | bytes 3145736 | tf_op jit(solution)/shard_map/ppermute | solution.py:109
  224.7 43.6 %collective-permute-start.32 = (bf16[4,128,1024]{2,1,0:T(8,128)(2,1)}, bf16[4,128,1024]{2,1,0:T(8,128)(2,1)}, u32[]{:S(2)}, u32[]{:S(2)}) collective-permute-start(bf16[4,128,1024]{2,1,0:T(8,128)(2,1)} %all-to-all-done.5.refs_0_), channel_id=1, source_target_pairs={{0,1},{1,0},{2,3},{3,2},{4,5},{5,4},{6,7},{7,6},{8,9},{9,8},{10,11... | collective-permute-start | bytes 3145736 | tf_op jit(solution)/shard_map/ppermute | solution.py:109
  225.4 41.1 %collective-permute-start.30 = (bf16[4,96,1024]{2,1,0:T(8,128)(2,1)}, bf16[4,96,1024]{2,1,0:T(8,128)(2,1)S(1)}, u32[]{:S(2)}, u32[]{:S(2)}) collective-permute-start(bf16[4,96,1024]{2,1,0:T(8,128)(2,1)} %slice.240), channel_id=1, source_target_pairs={{0,4},{4,0},{1,5},{5,1},{2,6},{6,2},{3,7},{7,3},{8,12},{12,8},{9,1... | collective-permute-start | bytes 2359304 | tf_op jit(solution)/shard_map/ppermute | solution.py:109
  251.9 27.8 %collective-permute-start.33 = (bf16[4,128,1024]{2,1,0:T(8,128)(2,1)}, bf16[4,128,1024]{2,1,0:T(8,128)(2,1)}, u32[]{:S(2)}, u32[]{:S(2)}) collective-permute-start(bf16[4,128,1024]{2,1,0:T(8,128)(2,1)} %collective-permute-done.28.refs_1_), channel_id=1, source_target_pairs={{0,1},{1,0},{2,3},{3,2},{4,5},{5,4},{6,7},{7,6},{8,9},{9,8},{10,11... | collective-permute-start | bytes 3145736 | tf_op jit(solution)/shard_map/ppermute | solution.py:109
  251.9 27.8 %collective-permute-start.34 = (bf16[4,128,1024]{2,1,0:T(8,128)(2,1)}, bf16[4,128,1024]{2,1,0:T(8,128)(2,1)}, u32[]{:S(2)}, u32[]{:S(2)}) collective-permute-start(bf16[4,128,1024]{2,1,0:T(8,128)(2,1)} %collective-permute-done.29.refs_2_), channel_id=1, source_target_pairs={{0,1},{1,0},{2,3},{3,2},{4,5},{5,4},{6,7},{7,6},{8,9},{9,8},{10,11... | collective-permute-start | bytes 3145736 | tf_op jit(solution)/shard_map/ppermute | solution.py:109
  253.3 49.4 %collective-permute-start.37 = (bf16[640,2048]{1,0:T(8,128)(2,1)}, bf16[640,2048]{1,0:T(8,128)(2,1)}, u32[]{:S(2)}, u32[]{:S(2)}) collective-permute-start(bf16[640,2048]{1,0:T(8,128)(2,1)} %fusion.20), channel_id=1, source_target_pairs={{0,1},{1,0},{2,3},{3,2},{4,5},{5,4},{6,7},{7,6},{8,9},{9,8},{10,11... | collective-permute-start | bytes 7864328 | tf_op jit(solution)/shard_map/ppermute | solution.py:109
  266.4 13.3 %collective-permute-start.35 = (bf16[4,96,1024]{2,1,0:T(8,128)(2,1)S(1)}, bf16[4,96,1024]{2,1,0:T(8,128)(2,1)}, u32[]{:S(2)}, u32[]{:S(2)}) collective-permute-start(bf16[4,96,1024]{2,1,0:T(8,128)(2,1)S(1)} %collective-permute-done.30.refs_3_), channel_id=1, source_target_pairs={{0,1},{1,0},{2,3},{3,2},{4,5},{5,4},{6,7},{7,6},{8,9},{9,8},{10,11... | collective-permute-start | bytes 2359304 | tf_op jit(solution)/shard_map/ppermute | solution.py:109
  279.6 23.1 %collective-permute-start.38 = (bf16[640,1024]{1,0:T(8,128)(2,1)}, bf16[640,1024]{1,0:T(8,128)(2,1)}, u32[]{:S(2)}, u32[]{:S(2)}) collective-permute-start(bf16[640,1024]{1,0:T(8,128)(2,1)} %bitcast_select_fusion.g_ref), channel_id=1, source_target_pairs={{0,1},{1,0},{2,3},{3,2},{4,5},{5,4},{6,7},{7,6},{8,9},{9,8},{10,11... | collective-permute-start | bytes 3932168 | tf_op jit(solution)/shard_map/ppermute | solution.py:109
  298.2 43.4 %all-to-all-start.6 = ((bf16[8,80,1024]{2,1,0:T(8,128)(2,1)}), bf16[8,80,1024]{2,1,0:T(8,128)(2,1)}, u32[]{:S(2)}, u32[]{:S(2)}) async-start(bf16[8,80,1024]{2,1,0:T(8,128)(2,1)} %bitcast.116), calls=%async_computation.6 | async-start | bytes 2621440 | tf_op jit(solution)/shard_map/all_to_all | solution.py:113
  313.1 20.4 %collective-permute-start.39 = (bf16[4,96,1024]{2,1,0:T(8,128)(2,1)S(1)}, bf16[4,96,1024]{2,1,0:T(8,128)(2,1)S(1)}, u32[]{:S(2)}, u32[]{:S(2)}) collective-permute-start(bf16[4,96,1024]{2,1,0:T(8,128)(2,1)S(1)} %get-tuple-element.55), channel_id=1, source_target_pairs={{0,4},{4,0},{1,5},{5,1},{2,6},{6,2},{3,7},{7,3},{8,12},{12,8},{9,1... | collective-permute-start | bytes 2359304 | tf_op jit(solution)/shard_map/ppermute | solution.py:109
  314.0 14.9 %collective-permute-start.40 = (bf16[4,32,1024]{2,1,0:T(8,128)(2,1)S(1)}, bf16[4,32,1024]{2,1,0:T(8,128)(2,1)S(1)}, u32[]{:S(2)}, u32[]{:S(2)}) collective-permute-start(bf16[4,32,1024]{2,1,0:T(8,128)(2,1)S(1)} %get-tuple-element.56), channel_id=1, source_target_pairs={{0,2},{2,0},{1,3},{3,1},{4,6},{6,4},{5,7},{7,5},{8,10},{10,8},{9,1... | collective-permute-start | bytes 786440 | tf_op jit(solution)/shard_map/ppermute | solution.py:109
  330.2 25.5 %collective-permute-start.44 = (bf16[4,128,1024]{2,1,0:T(8,128)(2,1)}, bf16[4,128,1024]{2,1,0:T(8,128)(2,1)}, u32[]{:S(2)}, u32[]{:S(2)}) collective-permute-start(bf16[4,128,1024]{2,1,0:T(8,128)(2,1)} %pad_maximum_fusion.1), channel_id=1, source_target_pairs={{0,4},{4,0},{1,5},{5,1},{2,6},{6,2},{3,7},{7,3},{8,12},{12,8},{9,1... | collective-permute-start | bytes 3145736 | tf_op jit(solution)/shard_map/ppermute | solution.py:109
  334.9 24.6 %collective-permute-start.43 = (bf16[4,128,1024]{2,1,0:T(8,128)(2,1)}, bf16[4,128,1024]{2,1,0:T(8,128)(2,1)}, u32[]{:S(2)}, u32[]{:S(2)}) collective-permute-start(bf16[4,128,1024]{2,1,0:T(8,128)(2,1)} %pad_maximum_fusion), channel_id=1, source_target_pairs={{0,2},{2,0},{1,3},{3,1},{4,6},{6,4},{5,7},{7,5},{8,10},{10,8},{9,1... | collective-permute-start | bytes 3145736 | tf_op jit(solution)/shard_map/ppermute | solution.py:109
  338.7 56.6 %collective-permute-start.42 = (bf16[640,2048]{1,0:T(8,128)(2,1)}, bf16[640,2048]{1,0:T(8,128)(2,1)}, u32[]{:S(2)}, u32[]{:S(2)}) collective-permute-start(bf16[640,2048]{1,0:T(8,128)(2,1)} %slice_select_fusion), channel_id=1, source_target_pairs={{0,1},{1,0},{2,3},{3,2},{4,5},{5,4},{6,7},{7,6},{8,9},{9,8},{10,11... | collective-permute-start | bytes 7864328 | tf_op jit(solution)/shard_map/ppermute | solution.py:109
  338.8 164.2 %collective-permute-start.55 = (bf16[640,1024]{1,0:T(8,128)(2,1)S(1)}, bf16[640,1024]{1,0:T(8,128)(2,1)}, u32[]{:S(2)}, u32[]{:S(2)}) collective-permute-start(bf16[640,1024]{1,0:T(8,128)(2,1)S(1)} %fusion.11.a_ref), channel_id=1, source_target_pairs={{0,1},{1,0},{2,3},{3,2},{4,5},{5,4},{6,7},{7,6},{8,9},{9,8},{10,11... | collective-permute-start | bytes 3932168 | tf_op jit(solution)/shard_map/ppermute | solution.py:109
  341.6 53.8 %collective-permute-start.41 = (bf16[640,1024]{1,0:T(8,128)(2,1)}, bf16[640,1024]{1,0:T(8,128)(2,1)}, u32[]{:S(2)}, u32[]{:S(2)}) collective-permute-start(bf16[640,1024]{1,0:T(8,128)(2,1)} %add_convert_fusion.1.a_ref), channel_id=1, source_target_pairs={{0,1},{1,0},{2,3},{3,2},{4,5},{5,4},{6,7},{7,6},{8,9},{9,8},{10,11... | collective-permute-start | bytes 3932168 | tf_op jit(solution)/shard_map/ppermute | solution.py:109
  355.7 73.2 %collective-permute-start.45 = (bf16[640,1024]{1,0:T(8,128)(2,1)S(1)}, bf16[640,1024]{1,0:T(8,128)(2,1)}, u32[]{:S(2)}, u32[]{:S(2)}) collective-permute-start(bf16[640,1024]{1,0:T(8,128)(2,1)S(1)} %bitcast.99), channel_id=1, source_target_pairs={{0,1},{1,0},{2,3},{3,2},{4,5},{5,4},{6,7},{7,6},{8,9},{9,8},{10,11... | collective-permute-start | bytes 3932168 | tf_op jit(solution)/shard_map/ppermute | solution.py:109
  363.0 29.6 %all-to-all-start.8 = ((bf16[4,128,1024]{2,1,0:T(8,128)(2,1)}), bf16[4,128,1024]{2,1,0:T(8,128)(2,1)}, u32[]{:S(2)}, u32[]{:S(2)}) async-start(bf16[4,128,1024]{2,1,0:T(8,128)(2,1)} %add_convert_fusion.3), calls=%async_computation.8 | async-start | bytes 2097152 | tf_op jit(solution)/shard_map/all_to_all | solution.py:113
  394.8 23.2 %collective-permute-start.70 = (bf16[128,1024]{1,0:T(8,128)(2,1)}, bf16[128,1024]{1,0:T(8,128)(2,1)S(1)}, u32[]{:S(2)}, u32[]{:S(2)}) collective-permute-start(bf16[128,1024]{1,0:T(8,128)(2,1)} %reduce_sum.221), channel_id=1, source_target_pairs={{0,2},{2,0},{1,3},{3,1},{4,6},{6,4},{5,7},{7,5},{8,10},{10,8},{9,1... | collective-permute-start | bytes 786440 | tf_op jit(solution)/shard_map/ppermute | solution.py:109
  413.9 15.1 %collective-permute-start.46 = (bf16[640,512]{1,0:T(8,128)(2,1)S(1)}, bf16[640,512]{1,0:T(8,128)(2,1)S(1)}, u32[]{:S(2)}, u32[]{:S(2)}) collective-permute-start(bf16[640,512]{1,0:T(8,128)(2,1)S(1)} %slice_select_fusion.2), channel_id=1, source_target_pairs={{0,1},{1,0},{2,3},{3,2},{4,5},{5,4},{6,7},{7,6},{8,9},{9,8},{10,11... | collective-permute-start | bytes 1966088 | tf_op jit(solution)/shard_map/ppermute | solution.py:109
  413.9 52.7 %collective-permute-start.47 = (bf16[4,48,2048]{2,1,0:T(8,128)(2,1)}, bf16[4,48,2048]{2,1,0:T(8,128)(2,1)}, u32[]{:S(2)}, u32[]{:S(2)}) collective-permute-start(bf16[4,48,2048]{2,1,0:T(8,128)(2,1)} %get-tuple-element.64), channel_id=1, source_target_pairs={{0,4},{4,0},{1,5},{5,1},{2,6},{6,2},{3,7},{7,3},{8,12},{12,8},{9,1... | collective-permute-start | bytes 2359304 | tf_op jit(solution)/shard_map/ppermute | solution.py:109
  427.5 85.0 %collective-permute-start.52 = (bf16[4,64,2048]{2,1,0:T(8,128)(2,1)}, bf16[4,64,2048]{2,1,0:T(8,128)(2,1)}, u32[]{:S(2)}, u32[]{:S(2)}) collective-permute-start(bf16[4,64,2048]{2,1,0:T(8,128)(2,1)} %pad_maximum_fusion.3), channel_id=1, source_target_pairs={{0,4},{4,0},{1,5},{5,1},{2,6},{6,2},{3,7},{7,3},{8,12},{12,8},{9,1... | collective-permute-start | bytes 3145736 | tf_op jit(solution)/shard_map/ppermute | solution.py:109
  433.3 31.7 %collective-permute-start.50 = (bf16[4,16,512]{2,1,0:T(8,128)(2,1)S(1)}, bf16[4,16,512]{2,1,0:T(8,128)(2,1)S(1)}, u32[]{:S(2)}, u32[]{:S(2)}) collective-permute-start(bf16[4,16,512]{2,1,0:T(8,128)(2,1)S(1)} %get-tuple-element.67), channel_id=1, source_target_pairs={{0,2},{2,0},{1,3},{3,1},{4,6},{6,4},{5,7},{7,5},{8,10},{10,8},{9,1... | collective-permute-start | bytes 196616 | tf_op jit(solution)/shard_map/ppermute | solution.py:109
  465.1 17.5 %collective-permute-start.54 = (bf16[4,64,512]{2,1,0:T(8,128)(2,1)S(1)}, bf16[4,64,512]{2,1,0:T(8,128)(2,1)S(1)}, u32[]{:S(2)}, u32[]{:S(2)}) collective-permute-start(bf16[4,64,512]{2,1,0:T(8,128)(2,1)S(1)} %pad_maximum_fusion.10), channel_id=1, source_target_pairs={{0,4},{4,0},{1,5},{5,1},{2,6},{6,2},{3,7},{7,3},{8,12},{12,8},{9,1... | collective-permute-start | bytes 786440 | tf_op jit(solution)/shard_map/ppermute | solution.py:109
  468.2 44.3 %collective-permute-start.51 = (bf16[4,64,2048]{2,1,0:T(8,128)(2,1)S(1)}, bf16[4,64,2048]{2,1,0:T(8,128)(2,1)}, u32[]{:S(2)}, u32[]{:S(2)}) collective-permute-start(bf16[4,64,2048]{2,1,0:T(8,128)(2,1)S(1)} %pad_maximum_fusion.2), channel_id=1, source_target_pairs={{0,2},{2,0},{1,3},{3,1},{4,6},{6,4},{5,7},{7,5},{8,10},{10,8},{9,1... | collective-permute-start | bytes 3145736 | tf_op jit(solution)/shard_map/ppermute | solution.py:109
  473.8 29.3 %collective-permute-start.56 = (bf16[640,1536]{1,0:T(8,128)(2,1)}, bf16[640,1536]{1,0:T(8,128)(2,1)}, u32[]{:S(2)}, u32[]{:S(2)}) collective-permute-start(bf16[640,1536]{1,0:T(8,128)(2,1)} %slice_select_fusion.1), channel_id=1, source_target_pairs={{0,1},{1,0},{2,3},{3,2},{4,5},{5,4},{6,7},{7,6},{8,9},{9,8},{10,11... | collective-permute-start | bytes 5898248 | tf_op jit(solution)/shard_map/ppermute | solution.py:109
  482.6 14.6 %collective-permute-start.53 = (bf16[4,64,512]{2,1,0:T(8,128)(2,1)S(1)}, bf16[4,64,512]{2,1,0:T(8,128)(2,1)S(1)}, u32[]{:S(2)}, u32[]{:S(2)}) collective-permute-start(bf16[4,64,512]{2,1,0:T(8,128)(2,1)S(1)} %pad_maximum_fusion.9), channel_id=1, source_target_pairs={{0,2},{2,0},{1,3},{3,1},{4,6},{6,4},{5,7},{7,5},{8,10},{10,8},{9,1... | collective-permute-start | bytes 786440 | tf_op jit(solution)/shard_map/ppermute | solution.py:109
  497.2 17.3 %collective-permute-start.71 = (bf16[256,1024]{1,0:T(8,128)(2,1)}, bf16[256,1024]{1,0:T(8,128)(2,1)}, u32[]{:S(2)}, u32[]{:S(2)}) collective-permute-start(bf16[256,1024]{1,0:T(8,128)(2,1)} %pad_maximum_fusion.7), channel_id=1, source_target_pairs={{0,1},{1,0},{2,3},{3,2},{4,5},{5,4},{6,7},{7,6},{8,9},{9,8},{10,11... | collective-permute-start | bytes 1572872 | tf_op jit(solution)/shard_map/ppermute | solution.py:109
  499.0 17.9 %all-to-all-start.12 = ((bf16[4,64,512]{2,1,0:T(8,128)(2,1)}), bf16[4,64,512]{2,1,0:T(8,128)(2,1)}, u32[]{:S(2)}, u32[]{:S(2)}) async-start(bf16[4,64,512]{2,1,0:T(8,128)(2,1)} %add_convert_fusion.8), calls=%async_computation.12 | async-start | bytes 524288 | tf_op jit(solution)/shard_map/all_to_all | solution.py:113
  518.0 55.4 %collective-permute-start.66 = (bf16[64,512]{1,0:T(8,128)(2,1)S(1)}, bf16[64,512]{1,0:T(8,128)(2,1)}, u32[]{:S(2)}, u32[]{:S(2)}) collective-permute-start(bf16[64,512]{1,0:T(8,128)(2,1)S(1)} %reduce_sum.219), channel_id=1, source_target_pairs={{0,2},{2,0},{1,3},{3,1},{4,6},{6,4},{5,7},{7,5},{8,10},{10,8},{9,1... | collective-permute-start | bytes 196616 | tf_op jit(solution)/shard_map/ppermute | solution.py:109
  524.1 18.4 %collective-permute-start.62 = (bf16[4,16,1536]{2,1,0:T(8,128)(2,1)S(1)}, bf16[4,16,1536]{2,1,0:T(8,128)(2,1)}, u32[]{:S(2)}, u32[]{:S(2)}) collective-permute-start(bf16[4,16,1536]{2,1,0:T(8,128)(2,1)S(1)} %copy-done.16), channel_id=1, source_target_pairs={{0,2},{2,0},{1,3},{3,1},{4,6},{6,4},{5,7},{7,5},{8,10},{10,8},{9,1... | collective-permute-start | bytes 589832 | tf_op jit(solution)/shard_map/ppermute | solution.py:109
  527.9 10.5 %all-to-all-start.10 = ((f32[4,1,1536]{2,1,0:T(1,128)}), f32[4,1,1536]{2,1,0:T(1,128)S(1)}, u32[]{:S(2)}, u32[]{:S(2)}) async-start(f32[4,1,1536]{2,1,0:T(1,128)} %all_to_all.59), calls=%async_computation.10 | async-start | bytes 49152 | tf_op jit(solution)/shard_map/all_to_all | solution.py:113
  534.3 15.5 %collective-permute-start.60 = (bf16[4,48,1536]{2,1,0:T(8,128)(2,1)S(1)}, bf16[4,48,1536]{2,1,0:T(8,128)(2,1)}, u32[]{:S(2)}, u32[]{:S(2)}) collective-permute-start(bf16[4,48,1536]{2,1,0:T(8,128)(2,1)S(1)} %copy-done.14), channel_id=1, source_target_pairs={{0,4},{4,0},{1,5},{5,1},{2,6},{6,2},{3,7},{7,3},{8,12},{12,8},{9,1... | collective-permute-start | bytes 1769480 | tf_op jit(solution)/shard_map/ppermute | solution.py:109
  539.0 26.7 %all-to-all-start.13 = ((bf16[4,64,2048]{2,1,0:T(8,128)(2,1)}), bf16[4,64,2048]{2,1,0:T(8,128)(2,1)S(1)}, u32[]{:S(2)}, u32[]{:S(2)}) async-start(bf16[4,64,2048]{2,1,0:T(8,128)(2,1)} %add_convert_fusion.2), calls=%async_computation.13 | async-start | bytes 2097152 | tf_op jit(solution)/shard_map/all_to_all | solution.py:113
  545.8 31.6 %collective-permute-start.63 = (bf16[4,64,1536]{2,1,0:T(8,128)(2,1)}, bf16[4,64,1536]{2,1,0:T(8,128)(2,1)}, u32[]{:S(2)}, u32[]{:S(2)}) collective-permute-start(bf16[4,64,1536]{2,1,0:T(8,128)(2,1)} %pad_maximum_fusion.5), channel_id=1, source_target_pairs={{0,4},{4,0},{1,5},{5,1},{2,6},{6,2},{3,7},{7,3},{8,12},{12,8},{9,1... | collective-permute-start | bytes 2359304 | tf_op jit(solution)/shard_map/ppermute | solution.py:109
  552.9 24.5 %collective-permute-start.61 = (bf16[4,64,1536]{2,1,0:T(8,128)(2,1)}, bf16[4,64,1536]{2,1,0:T(8,128)(2,1)}, u32[]{:S(2)}, u32[]{:S(2)}) collective-permute-start(bf16[4,64,1536]{2,1,0:T(8,128)(2,1)} %pad_maximum_fusion.4), channel_id=1, source_target_pairs={{0,2},{2,0},{1,3},{3,1},{4,6},{6,4},{5,7},{7,5},{8,10},{10,8},{9,1... | collective-permute-start | bytes 2359304 | tf_op jit(solution)/shard_map/ppermute | solution.py:109
  566.6 21.5 %all-to-all-start.9 = ((bf16[8,80,1024]{2,1,0:T(8,128)(2,1)}), bf16[8,80,1024]{2,1,0:T(8,128)(2,1)S(1)}, u32[]{:S(2)}, u32[]{:S(2)}) async-start(bf16[8,80,1024]{2,1,0:T(8,128)(2,1)} %bitcast.117), calls=%async_computation.9 | async-start | bytes 2621440 | tf_op jit(solution)/shard_map/all_to_all | solution.py:113
  574.9 20.2 %collective-permute-start.67 = (bf16[128,512]{1,0:T(8,128)(2,1)}, bf16[128,512]{1,0:T(8,128)(2,1)}, u32[]{:S(2)}, u32[]{:S(2)}) collective-permute-start(bf16[128,512]{1,0:T(8,128)(2,1)} %pad_maximum_fusion.11), channel_id=1, source_target_pairs={{0,1},{1,0},{2,3},{3,2},{4,5},{5,4},{6,7},{7,6},{8,9},{9,8},{10,11... | collective-permute-start | bytes 393224 | tf_op jit(solution)/shard_map/ppermute | solution.py:109
  575.6 17.7 %collective-permute-start.68 = (bf16[64,2048]{1,0:T(8,128)(2,1)S(1)}, bf16[64,2048]{1,0:T(8,128)(2,1)S(1)}, u32[]{:S(2)}, u32[]{:S(2)}) collective-permute-start(bf16[64,2048]{1,0:T(8,128)(2,1)S(1)} %reduce_sum.220), channel_id=1, source_target_pairs={{0,2},{2,0},{1,3},{3,1},{4,6},{6,4},{5,7},{7,5},{8,10},{10,8},{9,1... | collective-permute-start | bytes 786440 | tf_op jit(solution)/shard_map/ppermute | solution.py:109
  588.2 23.2 %all-to-all-start.11 = ((bf16[4,64,1536]{2,1,0:T(8,128)(2,1)}), bf16[4,64,1536]{2,1,0:T(8,128)(2,1)S(1)}, u32[]{:S(2)}, u32[]{:S(2)}) async-start(bf16[4,64,1536]{2,1,0:T(8,128)(2,1)} %add_convert_fusion.4), calls=%async_computation.11 | async-start | bytes 1572864 | tf_op jit(solution)/shard_map/all_to_all | solution.py:113
  595.1 17.0 %collective-permute-start.69 = (bf16[128,2048]{1,0:T(8,128)(2,1)}, bf16[128,2048]{1,0:T(8,128)(2,1)S(1)}, u32[]{:S(2)}, u32[]{:S(2)}) collective-permute-start(bf16[128,2048]{1,0:T(8,128)(2,1)} %pad_maximum_fusion.6), channel_id=1, source_target_pairs={{0,1},{1,0},{2,3},{3,2},{4,5},{5,4},{6,7},{7,6},{8,9},{9,8},{10,11... | collective-permute-start | bytes 1572872 | tf_op jit(solution)/shard_map/ppermute | solution.py:109
  (106 other events, 1198.8 us)
